TPU v7x, 32 devices: a whole 2x2x4 slice. The times are simulated.
32 devices in a mesh: grow: 8 (over z, y), lat: 4 (over x, core).
Axes of the slice: x: 2, y: 2, z: 4, core: 2. Of those that a mesh axis runs over, the one named last changes fastest.
Arguments:
- labels: int32 [128, 128, 128], P('grow', 'lat'), may hold values from 0 to 3
- roughness: float32 [4, 128, 128, 128], P(None, 'grow', 'lat'), may hold values from 0.1 to 1
- potential: float32 [2, 128, 128, 128], P(None, 'grow', 'lat'), may hold values from -3 to 3
- grad_coef: float32 [4, 3], replicated, may hold values from 0.2 to 1
- composition: float32 [4, 2], replicated, may hold values from -2 to 2
- latent: float32 [4], replicated, may hold values from 0.5 to 2
- diffusivity: float32 [2], replicated, may hold values from 0.5 to 2
- melt_table: float32 [16, 2], replicated, may hold values from -1 to 1
- melt_index: int32 [4, 8, 128, 128], P(None, None, 'lat'), may hold values from 0 to 15
Outputs:
- phases: float32 [4, 128, 128, 128], P(None, 'grow', 'lat')
- potentials: float32 [2, 128, 128, 128], P(None, 'grow', 'lat')
All inputs are finite; a program needn't handle non-finite values.
Results may differ from a plain program's by a relative error of at most 0.00025.
Values sent between devices are 32-bit elements; how exact they have to be, the bound alone decides.
No kernel may reach another device: no remote copies, remote signals or barrier semaphores. Data moves between devices by JAX's collectives and lax.ppermute only.
A program may use at most 64 MiB of HBM per device.

v0:
```python
import functools

import jax
import jax.numpy as jnp
from jax import lax
from jax.experimental import pallas as pl
from jax.experimental.pallas import tpu as pltpu
from jax.sharding import PartitionSpec as P


STEPS = 4
ROUNDS = 4
SHIFT = 8
SENT = (0, 1, 2, 4, 5)
PAD = 8
DT = 0.04
PLANES = (4, 3, 2, 1)
AXES = ("grow", "lat")
GRAD, CENTER, COUPLE, LATENT, RELEASE, SPREAD, STAY, MELT = 0, 12, 16, 24, 28, 36, 38, 40


def scalar_table(grad_coef, composition, latent, diffusivity, melt_table):
    scaled = DT * grad_coef
    return jnp.concatenate(
        [
            scaled.reshape(-1),
            1.0 + DT - 2.0 * jnp.sum(scaled, axis=1),
            (DT * (composition - jnp.mean(composition, axis=0))).reshape(-1),
            DT * (latent - jnp.mean(latent)),
            (composition - composition[3]).reshape(-1),
            DT * diffusivity,
            1.0 - 6.0 * DT * diffusivity,
            melt_table.reshape(-1),
        ]
    )


class Round:
    def __init__(self, turn, place, sizes, table, even, odd):
        self.ng, self.block, self.rows = sizes
        self.table, self.levels = table, (even, odd, even, odd)
        self.start = place * self.block + SHIFT * (turn + 1) - STEPS
        self.lowest = SHIFT * turn - self.start
        self.top = self.ng * self.block + SHIFT * turn - 1 - self.start

    def fill(self, source, halo, planes, to, halo_from, source_from):
        level = self.levels[0]

        @pl.loop(0, planes)
        def _(i):
            body = [source[f, i + source_from] for f in range(len(SENT))]
            side = [halo[f, i + halo_from] for f in range(len(SENT))]
            body.insert(3, 1.0 - body[0] - body[1] - body[2])
            side.insert(3, 1.0 - side[0] - side[1] - side[2])
            for f in range(6):
                level[f, i + to, PAD : PAD + self.rows] = body[f]
                level[f, i + to, PAD - STEPS : PAD] = side[f][:STEPS]
                level[f, i + to, PAD + self.rows : PAD + self.rows + STEPS] = side[f][STEPS:]

    def advance(self, src, e, at):
        table, window = self.table, pl.ds(at, 8)
        up, down = jnp.minimum(e + 1, self.top), jnp.maximum(e - 1, self.lowest)
        total = float(self.ng * self.block)
        theta = ((e + self.start).astype(jnp.float32) - 0.5 * total) / total
        mid = [src[f, e, window] for f in range(6)]
        gsum = [src[f, up, window] + src[f, down, window] for f in range(6)]
        xsum = [src[f, e, pl.ds(at + 1, 8)] + src[f, e, pl.ds(at - 1, 8)] for f in range(6)]
        ysum = [pltpu.roll(v, 1, 1) + pltpu.roll(v, v.shape[1] - 1, 1) for v in mid]
        spread = [
            table[GRAD + 3 * a] * gsum[a]
            + table[GRAD + 3 * a + 1] * xsum[a]
            + table[GRAD + 3 * a + 2] * ysum[a]
            + table[CENTER + a] * mid[a]
            for a in range(4)
        ]
        mean = 0.25 * (spread[0] + spread[1] + spread[2] + spread[3]) - 0.25
        trial = [
            spread[a]
            - mean
            - table[COUPLE + 2 * a] * mid[4]
            - table[COUPLE + 2 * a + 1] * mid[5]
            - table[LATENT + a] * theta
            for a in range(3)
        ]
        trial.append(1.0 - trial[0] - trial[1] - trial[2])
        clipped = [jnp.clip(t, 0.0, 1.0) for t in trial]
        inverse = 1.0 / (clipped[0] + clipped[1] + clipped[2] + clipped[3])
        new = [c * inverse for c in clipped]
        change = [n - v for n, v in zip(new[:3], mid[:3])]
        for k in range(2):
            release = table[RELEASE + k] * change[0]
            for a in range(1, 3):
                release = release + table[RELEASE + 2 * a + k] * change[a]
            sides = gsum[4 + k] + xsum[4 + k] + ysum[4 + k]
            new.append(table[SPREAD + k] * sides + table[STAY + k] * mid[4 + k] - release)
        return new

    def sweep(self, step, first, stop, write=None):
        src, dst = self.levels[step - 1], self.levels[step % STEPS]
        if write is None:
            tiles = [PAD - STEPS + 8 * t for t in range(self.rows // 8 + 1)]

            def write(e, at, new):
                for f in range(6):
                    dst[f, e, pl.ds(at, 8)] = new[f]

        else:
            tiles = [PAD + 8 * t for t in range(self.rows // 8)]

        many = next(n for n in PLANES if (stop - first) % n == 0)

        @pl.loop(0, (stop - first) // many)
        def _(i):
            for p in range(many):
                e = first + many * i + p
                for at in tiles:
                    write(e, at, self.advance(src, e, at))


def part_kernel(turn, place_of, sizes, begin, parts, has_seam, gives_seam, out_from, fresh, table, *refs):
    refs, (even, odd) = list(refs[:-2]), refs[-2:]
    place = place_of()
    run = Round(turn, place, sizes, table, even, odd)
    end = begin
    seam = refs.pop(0) if has_seam else None
    index = refs.pop(0) if fresh else None
    halo = refs.pop(0)
    for planes, halo_from, source_from in parts:
        run.fill(refs.pop(0), halo, planes, end, halo_from, source_from)
        end += planes
    next_seam = refs.pop() if gives_seam else None
    outs = [(ref, o + STEPS, o + STEPS + ref.shape[1]) for ref, o in zip(refs, out_from)]

    def bounds(step):
        return (begin if has_seam else 2 * step) - step, end - step

    def hold(level):
        if gives_seam:
            for plane in range(2):
                for f in range(6):
                    next_seam[level, f, plane] = run.levels[level][f, end - level - 2 + plane]

    def write(first, stop):
        targets = [(ref, at) for ref, at, until in outs if at <= first and stop <= until]

        def put(e, at, new):
            for ref, origin in targets:
                for i, f in enumerate(SENT):
                    ref[i, e - origin, pl.ds(at - PAD, 8)] = new[f]

        return put

    if has_seam:
        for level in range(STEPS):
            for plane in range(2):
                for f in range(6):
                    run.levels[level][f, begin - level - 2 + plane] = seam[level, f, plane]
    hold(0)
    for step in range(1, STEPS):
        run.sweep(step, *bounds(step))
        hold(step)
    marks = sorted(set(bounds(STEPS)) | set(m for _, *ends in outs for m in ends))
    for first, stop in zip(marks, marks[1:]):
        run.sweep(STEPS, first, stop, write(first, stop))

    if fresh:

        @pl.when(place == run.ng - 1)
        def _():
            for j in range(SHIFT):
                e = run.block - SHIFT + j + STEPS
                if any(at <= e < until for _, at, until in outs):
                    for t in range(run.rows // 8):
                        write(e, e + 1)(e, PAD + 8 * t, melt(table, index[turn, j, pl.ds(8 * t, 8)]))


def melt(table, row):
    mu = [jnp.zeros(row.shape, jnp.float32)] * 2
    for m in range((table.shape[0] - MELT) // 2):
        mu = [jnp.where(row == m, table[MELT + 2 * m + k], mu[k]) for k in range(2)]
    none = jnp.zeros(row.shape, jnp.float32)
    return [none, none, none, none + 1.0] + mu


def finish_kernel(place_of, ng, turn, table, index, *refs):
    pieces, (phases, potentials) = refs[:-2], refs[-2:]

    def put(o, here, new):
        for a in range(4):
            phases[a, o, here] = new[a]
        for k in range(2):
            potentials[k, o, here] = new[4 + k]

    at = 0
    for part in pieces:

        @pl.loop(0, part.shape[1])
        def _(i, part=part, at=at):
            new = [part[f, i] for f in range(len(SENT))]
            new.insert(3, 1.0 - new[0] - new[1] - new[2])
            put(i + at, slice(None), new)

        at += part.shape[1]

    @pl.when(place_of() == ng - 1)
    def _():
        for j in range(SHIFT):
            for t in range(index.shape[2] // 8):
                here = pl.ds(8 * t, 8)
                put(at - SHIFT + j, here, melt(table, index[turn, j, here]))


def prepare_kernel(labels_in, roughness_in, potential_in, *refs):
    outs, (first_rows, final_rows), (labels, roughness, potential, sems) = refs[:-6], refs[-6:-4], refs[-4:]
    rows = labels.shape[1]
    starts = (0, outs[0].shape[1])
    ranges = [(ref, at, at + ref.shape[1]) for ref, at in zip(outs, starts)]
    marks = sorted(set(m for _, *ends in ranges for m in ends))
    copies = []
    for n, (first, stop) in enumerate(zip(marks, marks[1:])):
        span = pl.ds(first, stop - first)
        pairs = [(labels_in.at[span], labels.at[span])]
        pairs += [(roughness_in.at[a, span], roughness.at[a, span]) for a in range(4)]
        pairs += [(potential_in.at[k, span], potential.at[k, span]) for k in range(2)]
        copies.append([pltpu.make_async_copy(*pair, sems.at[n, i]) for i, pair in enumerate(pairs)])
        for copy in copies[-1]:
            copy.start()
    for n, (first, stop) in enumerate(zip(marks, marks[1:])):
        targets = [(ref, at) for ref, at, until in ranges if at <= first and stop <= until]
        for copy in copies[n]:
            copy.wait()

        @pl.loop(first, stop)
        def _(o, targets=targets):
            kind = labels[o]
            rough = [roughness[a, o] for a in range(4)]
            inverse = 1.0 / (3.0 + rough[0] + rough[1] + rough[2] + rough[3])
            new = [(jnp.where(kind == a, 3.0, 0.0) + rough[a]) * inverse for a in range(3)]
            new += [potential[0, o], potential[1, o]]
            for f, value in enumerate(new):
                for ref, at in targets:
                    ref[f, o - at] = value
                first_rows[f, o] = value[:STEPS]
                final_rows[f, o] = value[rows - STEPS :]


def on_device(ng, nl, labels, roughness, potential, grad_coef, composition, latent, diffusivity, melt_table, melt_index):
    block, rows, lanes = labels.shape
    vmem = pl.BlockSpec(memory_space=pltpu.VMEM)
    smem = pl.BlockSpec(memory_space=pltpu.SMEM)
    f32 = jnp.float32
    kept = block - SHIFT + STEPS
    lows = block - kept
    highs = SHIFT + STEPS - lows
    height = kept + lows + highs
    table = scalar_table(grad_coef, composition, latent, diffusivity, melt_table)

    def home(g, l):
        return g * nl + l

    def away(g, l):
        return (g // 2 * 2 + (l % 2 ^ (l // 2 % 2))) * nl + l // 2 * 2 + g % 2

    def home_place():
        return lax.axis_index("grow")

    def away_place():
        return lax.axis_index("grow") // 2 * 2 + lax.axis_index("lat") % 2

    blocks = [(g, l) for g in range(ng) for l in range(nl)]

    def moved(array, before, after, climb):
        route = [(before(g + climb, l), after(g, l)) for g, l in blocks if g + climb < ng]
        return lax.ppermute(array, AXES, route)

    def edges(parts):
        first = jnp.concatenate([p[:, :, :STEPS] for p in parts], axis=1)
        final = jnp.concatenate([p[:, :, rows - STEPS :] for p in parts], axis=1)
        return first, final

    def beside(first, final, where):
        left = lax.ppermute(final, AXES, [(where(g, l), where(g, (l + 1) % nl)) for g, l in blocks])
        right = lax.ppermute(first, AXES, [(where(g, (l + 1) % nl), where(g, l)) for g, l in blocks])
        return left, right

    def piece(planes, width=rows):
        return jax.ShapeDtypeStruct((len(SENT), planes, width, lanes), f32)

    def cost(planes, moved_bytes):
        return pl.CostEstimate(flops=130 * 6 * planes * rows * lanes, bytes_accessed=moved_bytes, transcendentals=0)

    seam_shape = jax.ShapeDtypeStruct((STEPS, 6, 2, rows + 2 * PAD, lanes), f32)
    scratch = [pltpu.VMEM((6, height, rows + 2 * PAD, lanes), f32)] * 2

    def limit(size):
        return pltpu.CompilerParams(vmem_limit_bytes=size << 20)

    def part(turn, begin, planes, has_seam, gives_seam, sent, fresh, *args):
        size = sum(n for n, _, _ in planes)
        return pl.pallas_call(
            functools.partial(
                part_kernel,
                turn,
                away_place,
                (ng, block, rows),
                begin,
                planes,
                has_seam,
                gives_seam,
                [o for o, _ in sent],
                fresh,
            ),
            out_shape=[piece(n) for _, n in sent] + [seam_shape] * gives_seam,
            in_specs=[smem] + [vmem] * len(args),
            out_specs=[vmem] * (len(sent) + gives_seam),
            scratch_shapes=scratch,
            compiler_params=limit(24),
            cost_estimate=cost(4 * size, 4000000),
            name="part",
        )(table, *args)

    away_index = lax.ppermute(
        melt_index, AXES, [(away(ng - 1, l) // nl * nl + l, away(ng - 1, l)) for l in range(nl)]
    )

    front, back, first_rows, final_rows = pl.pallas_call(
        prepare_kernel,
        out_shape=[piece(highs), piece(block - highs)] + [piece(block, STEPS)] * 2,
        in_specs=[pl.BlockSpec(memory_space=pltpu.HBM)] * 3,
        out_specs=[vmem] * 4,
        scratch_shapes=[
            pltpu.VMEM(labels.shape, jnp.int32),
            pltpu.VMEM(roughness.shape, f32),
            pltpu.VMEM(potential.shape, f32),
            pltpu.SemaphoreType.DMA((2, 7)),
        ],
        compiler_params=limit(58),
        name="prepare",
    )(labels, roughness, potential)

    def packed(left, right, first, stop):
        return jnp.concatenate([left[:, first:stop], right[:, first:stop]], axis=2)

    front = moved(front, home, away, 0)
    left, right = beside(first_rows, final_rows, home)
    back = moved(back, home, away, 0)
    sides = moved(packed(left, right, 0, block), home, away, 0)
    above = moved(front, away, away, 1)
    above2 = moved(back[:, :lows], away, away, 1)
    halo = moved(sides, away, away, 1)
    early, seam = part(
        0,
        0,
        [(highs - lows, lows, lows), (block - highs, highs, 0)],
        False,
        True,
        [(0, lows)],
        False,
        sides,
        front,
        back,
    )
    low = moved(early, away, away, 1)
    high, rest = part(
        0,
        kept,
        [(highs, 0, 0), (lows, highs, 0)],
        True,
        False,
        [(lows, highs), (lows + highs, lows)],
        True,
        seam,
        away_index,
        halo,
        above,
        above2,
    )

    own_parts = [(highs, 0, 0), (lows, highs, 0)]
    for turn in range(1, ROUNDS):
        last = turn == ROUNDS - 1
        left, right = beside(*edges([early, high, rest]), away)
        own, own_halo = [high, rest], packed(left, right, lows, block)
        above = moved(high, away, away, 1)
        halo = moved(packed(left, right, 0, lows + highs), away, away, 1)
        early, seam = part(turn, 0, own_parts, False, True, [(0, lows)], False, own_halo, *own)
        sent = moved(early, away, home if last else away, 0 if last else 1)
        if last:
            break
        high, rest = part(
            turn,
            kept,
            [(lows, 0, 0), (highs, lows, 0)],
            True,
            False,
            [(lows, highs), (lows + highs, lows)],
            True,
            seam,
            away_index,
            halo,
            low,
            above,
        )
        low = sent

    cut = 2
    middle, seam = part(
        turn,
        kept,
        [(lows, 0, 0), (cut, lows, 0)],
        True,
        True,
        [(lows, lows + cut)],
        False,
        seam,
        halo,
        low,
        above,
    )
    middle = moved(middle, away, home, 0)
    (final,) = part(
        turn,
        kept + lows + cut,
        [(highs - cut, lows + cut, cut)],
        True,
        False,
        [(2 * lows + cut, highs - cut)],
        False,
        seam,
        halo,
        above,
    )
    final = moved(final, away, home, 0)
    return pl.pallas_call(
        functools.partial(finish_kernel, home_place, ng, turn),
        out_shape=[jax.ShapeDtypeStruct((n, block, rows, lanes), f32) for n in (4, 2)],
        in_specs=[smem] + [vmem] * 4,
        out_specs=[vmem] * 2,
        compiler_params=limit(8),
        name="finish",
    )(table, melt_index, sent, middle, final)


def solution(mesh):
    ng, nl = mesh.shape["grow"], mesh.shape["lat"]
    placed = (
        P("grow", "lat", None),
        P(None, "grow", "lat", None),
        P(None, "grow", "lat", None),
        P(),
        P(),
        P(),
        P(),
        P(),
        P(None, None, "lat", None),
    )
    return jax.shard_map(
        functools.partial(on_device, ng, nl),
        mesh=mesh,
        in_specs=placed,
        out_specs=(P(None, "grow", "lat", None), P(None, "grow", "lat", None)),
        check_vma=False,
    )
```

profile of v0, /device:TPU:17, one launch (start us, length us, event | category | flops | bytes accessed | tf_op | source)
XLA Modules:
  0.0 138.2 jit_solution(3600906680085360943)
XLA Ops:
  0.7 3.0 %prepare.1 = (f32[5,8,32,128]{3,2,1,0:T(8,128)}, f32[5,8,32,128]{3,2,1,0:T(8,128)}, f32[5,16,4,128]{3,2,1,0:T(4,128)}, f32[5,16,4,128]{3,2,1,0:T(4,128)}) custom-call(s32[16,32,128]{2,1,0:T(8,128)} %labels_in.1, f32[4,16,32,128]{3,2,1,0:T(8,128)} %roughness_in.1, f32[2,16,32,128]{3,2,1,0:T(8,128)} %potential_in.1), custom_call_target="tpu_custom_call" | custom-call | tf_op jit(solution)/shard_map/prepare/pallas_call | solution.py:326
  5.5 2.8 %collective-permute-start.3 = (f32[5,8,32,128]{3,2,1,0:T(8,128)}, f32[5,8,32,128]{3,2,1,0:T(8,128)S(1)}, u32[]{:S(2)}, u32[]{:S(2)}) collective-permute-start(f32[5,8,32,128]{3,2,1,0:T(8,128)} %get-tuple-element.24), channel_id=1, source_target_pairs={{0,0},{1,4},{2,6},{3,2},{4,1},{5,5},{6,7},{7,3},{8,8},{9,12},{10,1... | collective-permute-start | bytes 1966088 | tf_op jit(solution)/shard_map/ppermute | solution.py:274
  8.3 2.8 %collective-permute-start.4 = (f32[5,8,32,128]{3,2,1,0:T(8,128)}, f32[5,8,32,128]{3,2,1,0:T(8,128)S(1)}, u32[]{:S(2)}, u32[]{:S(2)}) collective-permute-start(f32[5,8,32,128]{3,2,1,0:T(8,128)} %get-tuple-element.25), channel_id=1, source_target_pairs={{0,0},{1,4},{2,6},{3,2},{4,1},{5,5},{6,7},{7,3},{8,8},{9,12},{10,1... | collective-permute-start | bytes 1966088 | tf_op jit(solution)/shard_map/ppermute | solution.py:274
  12.4 2.8 %collective-permute-start.2 = (f32[5,16,8,128]{3,2,1,0:T(8,128)S(1)}, f32[5,16,8,128]{3,2,1,0:T(8,128)}, u32[]{:S(2)}, u32[]{:S(2)}) collective-permute-start(f32[5,16,8,128]{3,2,1,0:T(8,128)S(1)} %pad_maximum_fusion), channel_id=1, source_target_pairs={{0,0},{1,4},{2,6},{3,2},{4,1},{5,5},{6,7},{7,3},{8,8},{9,12},{10,1... | collective-permute-start | bytes 983048 | tf_op jit(solution)/shard_map/ppermute | solution.py:274
  17.6 1.9 %collective-permute-start.7 = (f32[5,8,32,128]{3,2,1,0:T(8,128)S(1)}, f32[5,8,32,128]{3,2,1,0:T(8,128)S(1)}, u32[]{:S(2)}, u32[]{:S(2)}) collective-permute-start(f32[5,8,32,128]{3,2,1,0:T(8,128)S(1)} %collective-permute-done.3.refs_1_), channel_id=1, source_target_pairs={{1,0},{5,4},{7,6},{3,2},{8,1},{12,5},{14,7},{10,3},{9,8},{13,12},{... | collective-permute-start | bytes 1966088 | tf_op jit(solution)/shard_map/ppermute | solution.py:274
  19.6 8.7 %collective-permute-done.2.refs_0_ = f32[5,16,8,128]{3,2,1,0:T(8,128)} collective-permute-done((f32[5,16,8,128]{3,2,1,0:T(8,128)S(1)}, f32[5,16,8,128]{3,2,1,0:T(8,128)}, u32[]{:S(2)}, u32[]{:S(2)}) %collective-permute-start.2) | collective-permute-done | bytes 327712 | tf_op jit(solution)/shard_map/ppermute | solution.py:274
  28.3 1.9 %collective-permute-start.6 = (f32[5,16,8,128]{3,2,1,0:T(8,128)}, f32[5,16,8,128]{3,2,1,0:T(8,128)S(1)}, u32[]{:S(2)}, u32[]{:S(2)}) collective-permute-start(f32[5,16,8,128]{3,2,1,0:T(8,128)} %collective-permute-done.2.refs_0_), channel_id=1, source_target_pairs={{1,0},{5,4},{7,6},{3,2},{8,1},{12,5},{14,7},{10,3},{9,8},{13,12},{... | collective-permute-start | bytes 983048 | tf_op jit(solution)/shard_map/ppermute | solution.py:274
  31.0 2.4 %collective-permute-start.8 = (f32[5,4,32,128]{3,2,1,0:T(8,128)}, f32[5,4,32,128]{3,2,1,0:T(8,128)}, u32[]{:S(2)}, u32[]{:S(2)}) collective-permute-start(f32[5,4,32,128]{3,2,1,0:T(8,128)} %slice.128), channel_id=1, source_target_pairs={{1,0},{5,4},{7,6},{3,2},{8,1},{12,5},{14,7},{10,3},{9,8},{13,12},{... | collective-permute-start | bytes 983048 | tf_op jit(solution)/shard_map/ppermute | solution.py:274
  34.1 4.1 %part.9 = (f32[5,4,32,128]{3,2,1,0:T(8,128)S(1)}, f32[4,6,2,48,128]{4,3,2,1,0:T(8,128)S(1)}) custom-call(f32[72]{0:T(128)S(1)} %concatenate.42.table, f32[5,16,8,128]{3,2,1,0:T(8,128)} %collective-permute-done.2.refs_0_, f32[5,8,32,128]{3,2,1,0:T(8,128)S(1)} %collective-permute-done.3.refs_1_, f32[5,8,32,128]{3,2,1,0:T(8,128)S(1)} %collective-permute-done.4.refs_2_), custom_call_target="tpu_custom_call" | custom-call | flops 153354240 | bytes 4000000 | tf_op jit(solution)/shard_map/part/pallas_call | solution.py:300
  38.3 2.2 %collective-permute-done.8.refs_4_ = f32[5,4,32,128]{3,2,1,0:T(8,128)} collective-permute-done((f32[5,4,32,128]{3,2,1,0:T(8,128)}, f32[5,4,32,128]{3,2,1,0:T(8,128)}, u32[]{:S(2)}, u32[]{:S(2)}) %collective-permute-start.8) | collective-permute-done | bytes 327712 | tf_op jit(solution)/shard_map/ppermute | solution.py:274
  40.5 5.8 %part.10 = (f32[5,8,32,128]{3,2,1,0:T(8,128)S(1)}, f32[5,4,32,128]{3,2,1,0:T(8,128)S(1)}) custom-call(f32[72]{0:T(128)S(1)} %concatenate.42.table, f32[4,6,2,48,128]{4,3,2,1,0:T(8,128)S(1)} %get-tuple-element.27.refs_0_, s32[4,8,32,128]{3,2,1,0:T(8,128)S(1)} %collective-permute-done.5.refs_1_, f32[5,16,8,128]{3,2,1,0:T(8,128)S(1)} %collective-permute-done.6.refs_2_, ...), custom_call_target="tpu_custom_call" | custom-call | flops 153354240 | bytes 4000000 | tf_op jit(solution)/shard_map/part/pallas_call | solution.py:300
  47.1 1.9 %collective-permute-start.12 = (f32[5,4,32,128]{3,2,1,0:T(8,128)S(1)}, f32[5,4,32,128]{3,2,1,0:T(8,128)S(1)}, u32[]{:S(2)}, u32[]{:S(2)}) collective-permute-start(f32[5,4,32,128]{3,2,1,0:T(8,128)S(1)} %get-tuple-element.26), channel_id=1, source_target_pairs={{1,0},{5,4},{7,6},{3,2},{8,1},{12,5},{14,7},{10,3},{9,8},{13,12},{... | collective-permute-start | bytes 983048 | tf_op jit(solution)/shard_map/ppermute | solution.py:274
  49.0 2.5 %collective-permute-start.13 = (f32[5,8,32,128]{3,2,1,0:T(8,128)S(1)}, f32[5,8,32,128]{3,2,1,0:T(8,128)S(1)}, u32[]{:S(2)}, u32[]{:S(2)}) collective-permute-start(f32[5,8,32,128]{3,2,1,0:T(8,128)S(1)} %get-tuple-element.28.refs_1_), channel_id=1, source_target_pairs={{1,0},{5,4},{7,6},{3,2},{8,1},{12,5},{14,7},{10,3},{9,8},{13,12},{... | collective-permute-start | bytes 1966088 | tf_op jit(solution)/shard_map/ppermute | solution.py:274
  52.5 4.8 %collective-permute-done.9 = f32[5,16,4,128]{3,2,1,0:T(4,128)S(1)} collective-permute-done((f32[5,16,4,128]{3,2,1,0:T(4,128)S(1)}, f32[5,16,4,128]{3,2,1,0:T(4,128)S(1)}, u32[]{:S(2)}, u32[]{:S(2)}) %collective-permute-start.9) | collective-permute-done | bytes 163872 | tf_op jit(solution)/shard_map/ppermute | solution.py:282
  57.4 2.8 %collective-permute-start.11 = (f32[5,12,8,128]{3,2,1,0:T(8,128)S(1)}, f32[5,12,8,128]{3,2,1,0:T(8,128)S(1)}, u32[]{:S(2)}, u32[]{:S(2)}) collective-permute-start(f32[5,12,8,128]{3,2,1,0:T(8,128)S(1)} %pad_maximum_fusion.2), channel_id=1, source_target_pairs={{1,0},{5,4},{7,6},{3,2},{8,1},{12,5},{14,7},{10,3},{9,8},{13,12},{... | collective-permute-start | bytes 737288 | tf_op jit(solution)/shard_map/ppermute | solution.py:274
  60.2 3.7 %part.11 = (f32[5,4,32,128]{3,2,1,0:T(8,128)S(1)}, f32[4,6,2,48,128]{4,3,2,1,0:T(8,128)S(1)}) custom-call(f32[72]{0:T(128)S(1)} %concatenate.42.table, f32[5,12,8,128]{3,2,1,0:T(8,128)S(1)} %pad_maximum_fusion.1.refs_0_, f32[5,8,32,128]{3,2,1,0:T(8,128)S(1)} %get-tuple-element.28.refs_1_, f32[5,4,32,128]{3,2,1,0:T(8,128)S(1)} %get-tuple-element.29.refs_2_), custom_call_target="tpu_custom_call" | custom-call | flops 153354240 | bytes 4000000 | tf_op jit(solution)/shard_map/part/pallas_call | solution.py:300
  65.3 5.4 %part.12 = (f32[5,8,32,128]{3,2,1,0:T(8,128)S(1)}, f32[5,4,32,128]{3,2,1,0:T(8,128)S(1)}) custom-call(f32[72]{0:T(128)S(1)} %concatenate.42.table, f32[4,6,2,48,128]{4,3,2,1,0:T(8,128)S(1)} %get-tuple-element.31.refs_0_, s32[4,8,32,128]{3,2,1,0:T(8,128)S(1)} %collective-permute-done.5.refs_1_, f32[5,12,8,128]{3,2,1,0:T(8,128)S(1)} %collective-permute-done.11.refs_2_, ...), custom_call_target="tpu_custom_call" | custom-call | flops 153354240 | bytes 4000000 | tf_op jit(solution)/shard_map/part/pallas_call | solution.py:300
  74.0 2.4 %collective-permute-start.18 = (f32[5,8,32,128]{3,2,1,0:T(8,128)S(1)}, f32[5,8,32,128]{3,2,1,0:T(8,128)S(1)}, u32[]{:S(2)}, u32[]{:S(2)}) collective-permute-start(f32[5,8,32,128]{3,2,1,0:T(8,128)S(1)} %get-tuple-element.32.refs_1_), channel_id=1, source_target_pairs={{1,0},{5,4},{7,6},{3,2},{8,1},{12,5},{14,7},{10,3},{9,8},{13,12},{... | collective-permute-start | bytes 1966088 | tf_op jit(solution)/shard_map/ppermute | solution.py:274
  76.8 5.5 %collective-permute-done.14 = f32[5,16,4,128]{3,2,1,0:T(4,128)S(1)} collective-permute-done((f32[5,16,4,128]{3,2,1,0:T(4,128)S(1)}, f32[5,16,4,128]{3,2,1,0:T(4,128)S(1)}, u32[]{:S(2)}, u32[]{:S(2)}) %collective-permute-start.14) | collective-permute-done | bytes 163872 | tf_op jit(solution)/shard_map/ppermute | solution.py:282
  82.4 3.0 %collective-permute-start.16 = (f32[5,12,8,128]{3,2,1,0:T(8,128)S(1)}, f32[5,12,8,128]{3,2,1,0:T(8,128)S(1)}, u32[]{:S(2)}, u32[]{:S(2)}) collective-permute-start(f32[5,12,8,128]{3,2,1,0:T(8,128)S(1)} %pad_maximum_fusion.4), channel_id=1, source_target_pairs={{1,0},{5,4},{7,6},{3,2},{8,1},{12,5},{14,7},{10,3},{9,8},{13,12},{... | collective-permute-start | bytes 737288 | tf_op jit(solution)/shard_map/ppermute | solution.py:274
  85.4 3.7 %part.13 = (f32[5,4,32,128]{3,2,1,0:T(8,128)S(1)}, f32[4,6,2,48,128]{4,3,2,1,0:T(8,128)S(1)}) custom-call(f32[72]{0:T(128)S(1)} %concatenate.42.table, f32[5,12,8,128]{3,2,1,0:T(8,128)S(1)} %pad_maximum_fusion.3.refs_0_, f32[5,8,32,128]{3,2,1,0:T(8,128)S(1)} %get-tuple-element.32.refs_1_, f32[5,4,32,128]{3,2,1,0:T(8,128)S(1)} %get-tuple-element.33.refs_2_), custom_call_target="tpu_custom_call" | custom-call | flops 153354240 | bytes 4000000 | tf_op jit(solution)/shard_map/part/pallas_call | solution.py:300
  90.3 5.4 %part.14 = (f32[5,8,32,128]{3,2,1,0:T(8,128)S(1)}, f32[5,4,32,128]{3,2,1,0:T(8,128)S(1)}) custom-call(f32[72]{0:T(128)S(1)} %concatenate.42.table, f32[4,6,2,48,128]{4,3,2,1,0:T(8,128)S(1)} %get-tuple-element.35.refs_0_, s32[4,8,32,128]{3,2,1,0:T(8,128)S(1)} %collective-permute-done.5.refs_1_, f32[5,12,8,128]{3,2,1,0:T(8,128)S(1)} %collective-permute-done.16.refs_2_, ...), custom_call_target="tpu_custom_call" | custom-call | flops 153354240 | bytes 4000000 | tf_op jit(solution)/shard_map/part/pallas_call | solution.py:300
  97.9 2.4 %collective-permute-start.24 = (f32[5,8,32,128]{3,2,1,0:T(8,128)S(1)}, f32[5,8,32,128]{3,2,1,0:T(8,128)S(1)}, u32[]{:S(2)}, u32[]{:S(2)}) collective-permute-start(f32[5,8,32,128]{3,2,1,0:T(8,128)S(1)} %get-tuple-element.36.refs_1_), channel_id=1, source_target_pairs={{1,0},{5,4},{7,6},{3,2},{8,1},{12,5},{14,7},{10,3},{9,8},{13,12},{... | collective-permute-start | bytes 1966088 | tf_op jit(solution)/shard_map/ppermute | solution.py:274
  101.8 4.3 %collective-permute-done.19 = f32[5,16,4,128]{3,2,1,0:T(4,128)S(1)} collective-permute-done((f32[5,16,4,128]{3,2,1,0:T(4,128)S(1)}, f32[5,16,4,128]{3,2,1,0:T(4,128)S(1)}, u32[]{:S(2)}, u32[]{:S(2)}) %collective-permute-start.19) | collective-permute-done | bytes 163872 | tf_op jit(solution)/shard_map/ppermute | solution.py:282
  106.2 2.8 %collective-permute-start.22 = (f32[5,12,8,128]{3,2,1,0:T(8,128)S(1)}, f32[5,12,8,128]{3,2,1,0:T(8,128)S(1)}, u32[]{:S(2)}, u32[]{:S(2)}) collective-permute-start(f32[5,12,8,128]{3,2,1,0:T(8,128)S(1)} %pad_maximum_fusion.6), channel_id=1, source_target_pairs={{1,0},{5,4},{7,6},{3,2},{8,1},{12,5},{14,7},{10,3},{9,8},{13,12},{... | collective-permute-start | bytes 737288 | tf_op jit(solution)/shard_map/ppermute | solution.py:274
  109.1 3.7 %part.15 = (f32[5,4,32,128]{3,2,1,0:T(8,128)S(1)}, f32[4,6,2,48,128]{4,3,2,1,0:T(8,128)S(1)}) custom-call(f32[72]{0:T(128)S(1)} %concatenate.42.table, f32[5,12,8,128]{3,2,1,0:T(8,128)S(1)} %pad_maximum_fusion.5.refs_0_, f32[5,8,32,128]{3,2,1,0:T(8,128)S(1)} %get-tuple-element.36.refs_1_, f32[5,4,32,128]{3,2,1,0:T(8,128)S(1)} %get-tuple-element.37.refs_2_), custom_call_target="tpu_custom_call" | custom-call | flops 153354240 | bytes 4000000 | tf_op jit(solution)/shard_map/part/pallas_call | solution.py:300
  114.2 3.3 %part.16 = (f32[5,6,32,128]{3,2,1,0:T(8,128)S(1)}, f32[4,6,2,48,128]{4,3,2,1,0:T(8,128)S(1)}) custom-call(f32[72]{0:T(128)S(1)} %concatenate.42.table, f32[4,6,2,48,128]{4,3,2,1,0:T(8,128)S(1)} %get-tuple-element.39.refs_0_, f32[5,12,8,128]{3,2,1,0:T(8,128)S(1)} %collective-permute-done.22.refs_1_, f32[5,4,32,128]{3,2,1,0:T(8,128)S(1)} %collective-permute-done.23.refs_2_, ...), custom_call_target="tpu_custom_call" | custom-call | flops 76677120 | bytes 4000000 | tf_op jit(solution)/shard_map/part/pallas_call | solution.py:300
  117.4 1.9 %collective-permute-start.25 = (f32[5,6,32,128]{3,2,1,0:T(8,128)S(1)}, f32[5,6,32,128]{3,2,1,0:T(8,128)S(1)}, u32[]{:S(2)}, u32[]{:S(2)}) collective-permute-start(f32[5,6,32,128]{3,2,1,0:T(8,128)S(1)} %get-tuple-element.40), channel_id=1, source_target_pairs={{0,0},{4,1},{6,2},{2,3},{1,4},{5,5},{7,6},{3,7},{8,8},{12,9},{14,1... | collective-permute-start | bytes 1474568 | tf_op jit(solution)/shard_map/ppermute | solution.py:274
  119.4 3.2 %part.17 = f32[5,6,32,128]{3,2,1,0:T(8,128)S(1)} custom-call(f32[72]{0:T(128)S(1)} %concatenate.42.table, f32[4,6,2,48,128]{4,3,2,1,0:T(8,128)S(1)} %get-tuple-element.41.refs_0_, f32[5,12,8,128]{3,2,1,0:T(8,128)S(1)} %collective-permute-done.22.refs_1_, f32[5,8,32,128]{3,2,1,0:T(8,128)S(1)} %collective-permute-done.24.refs_3_.refs_2_), custom_call_target="tpu_custom_call" | custom-call | flops 76677120 | bytes 4000000 | tf_op jit(solution)/shard_map/part/pallas_call | solution.py:300
  122.6 3.6 %collective-permute-start.26 = (f32[5,6,32,128]{3,2,1,0:T(8,128)S(1)}, f32[5,6,32,128]{3,2,1,0:T(8,128)S(1)}, u32[]{:S(2)}, u32[]{:S(2)}) collective-permute-start(f32[5,6,32,128]{3,2,1,0:T(8,128)S(1)} %part.17), channel_id=1, source_target_pairs={{0,0},{4,1},{6,2},{2,3},{1,4},{5,5},{7,6},{3,7},{8,8},{12,9},{14,1... | collective-permute-start | bytes 1474568 | tf_op jit(solution)/shard_map/ppermute | solution.py:274
  126.2 1.9 %collective-permute-start.21 = (f32[5,4,32,128]{3,2,1,0:T(8,128)S(1)}, f32[5,4,32,128]{3,2,1,0:T(8,128)S(1)}, u32[]{:S(2)}, u32[]{:S(2)}) collective-permute-start(f32[5,4,32,128]{3,2,1,0:T(8,128)S(1)} %get-tuple-element.38), channel_id=1, source_target_pairs={{0,0},{4,1},{6,2},{2,3},{1,4},{5,5},{7,6},{3,7},{8,8},{12,9},{14,1... | collective-permute-start | bytes 983048 | tf_op jit(solution)/shard_map/ppermute | solution.py:274
  128.2 8.2 %collective-permute-done.21.refs_0_ = f32[5,4,32,128]{3,2,1,0:T(8,128)S(1)} collective-permute-done((f32[5,4,32,128]{3,2,1,0:T(8,128)S(1)}, f32[5,4,32,128]{3,2,1,0:T(8,128)S(1)}, u32[]{:S(2)}, u32[]{:S(2)}) %collective-permute-start.21) | collective-permute-done | bytes 327712 | tf_op jit(solution)/shard_map/ppermute | solution.py:274
  (90 shorter events, 21.6 us)
Async XLA Ops:
  0.6 11.2 %copy-start.2 = (f32[4,3]{1,0:T(4,128)S(1)}, f32[4,3]{1,0:T(4,128)}, u32[]{:S(2)}) copy-start(f32[4,3]{1,0:T(4,128)} %param.12) | copy-start | bytes 148
  0.7 11.3 %copy-start.1 = (f32[4,2]{0,1:T(2,128)S(1)}, f32[4,2]{0,1:T(2,128)}, u32[]{:S(2)}) copy-start(f32[4,2]{0,1:T(2,128)} %param.13) | copy-start | bytes 100
  0.7 14.6 %copy-start.4 = (f32[4]{0:T(128)S(1)}, f32[4]{0:T(128)}, u32[]{:S(2)}) copy-start(f32[4]{0:T(128)} %param.14) | copy-start | bytes 52
  0.7 32.7 %copy-start.5 = (f32[2]{0:T(128)S(1)}, f32[2]{0:T(128)}, u32[]{:S(2)}) copy-start(f32[2]{0:T(128)} %param.15) | copy-start | bytes 28
  0.7 33.2 %copy-start.3 = (f32[16,2]{0,1:T(2,128)S(1)}, f32[16,2]{0,1:T(2,128)}, u32[]{:S(2)}) copy-start(f32[16,2]{0,1:T(2,128)} %param.16) | copy-start | bytes 388
  3.7 8.6 %collective-permute-start.1 = (f32[5,16,4,128]{3,2,1,0:T(4,128)}, f32[5,16,4,128]{3,2,1,0:T(4,128)S(1)}, u32[]{:S(2)}, u32[]{:S(2)}) collective-permute-start(f32[5,16,4,128]{3,2,1,0:T(4,128)} %get-tuple-element.23), channel_id=1, source_target_pairs={{1,0},{2,1},{3,2},{0,3},{5,4},{6,5},{7,6},{4,7},{9,8},{10,9},{11,1... | collective-permute-start | bytes 491528 | tf_op jit(solution)/shard_map/ppermute | solution.py:283
  4.4 7.9 %collective-permute-start = (f32[5,16,4,128]{3,2,1,0:T(4,128)}, f32[5,16,4,128]{3,2,1,0:T(4,128)S(1)}, u32[]{:S(2)}, u32[]{:S(2)}) collective-permute-start(f32[5,16,4,128]{3,2,1,0:T(4,128)} %get-tuple-element.22), channel_id=1, source_target_pairs={{0,1},{1,2},{2,3},{3,0},{4,5},{5,6},{6,7},{7,4},{8,9},{9,10},{10,1... | collective-permute-start | bytes 491528 | tf_op jit(solution)/shard_map/ppermute | solution.py:282
  5.5 12.1 %collective-permute-start.3 = (f32[5,8,32,128]{3,2,1,0:T(8,128)}, f32[5,8,32,128]{3,2,1,0:T(8,128)S(1)}, u32[]{:S(2)}, u32[]{:S(2)}) collective-permute-start(f32[5,8,32,128]{3,2,1,0:T(8,128)} %get-tuple-element.24), channel_id=1, source_target_pairs={{0,0},{1,4},{2,6},{3,2},{4,1},{5,5},{6,7},{7,3},{8,8},{9,12},{10,1... | collective-permute-start | bytes 1966088 | tf_op jit(solution)/shard_map/ppermute | solution.py:274
  8.3 21.9 %collective-permute-start.4 = (f32[5,8,32,128]{3,2,1,0:T(8,128)}, f32[5,8,32,128]{3,2,1,0:T(8,128)S(1)}, u32[]{:S(2)}, u32[]{:S(2)}) collective-permute-start(f32[5,8,32,128]{3,2,1,0:T(8,128)} %get-tuple-element.25), channel_id=1, source_target_pairs={{0,0},{1,4},{2,6},{3,2},{4,1},{5,5},{6,7},{7,3},{8,8},{9,12},{10,1... | collective-permute-start | bytes 1966088 | tf_op jit(solution)/shard_map/ppermute | solution.py:274
  11.1 27.2 %collective-permute-start.5 = (s32[4,8,32,128]{3,2,1,0:T(8,128)S(1)}, s32[4,8,32,128]{3,2,1,0:T(8,128)S(1)}, u32[]{:S(2)}, u32[]{:S(2)}) collective-permute-start(s32[4,8,32,128]{3,2,1,0:T(8,128)S(1)} %copy-done), channel_id=1, source_target_pairs={{24,25},{29,29},{30,31},{27,27}} | collective-permute-start | bytes 1572872 | tf_op jit(solution)/shard_map/ppermute | solution.py:322
  12.4 15.9 %collective-permute-start.2 = (f32[5,16,8,128]{3,2,1,0:T(8,128)S(1)}, f32[5,16,8,128]{3,2,1,0:T(8,128)}, u32[]{:S(2)}, u32[]{:S(2)}) collective-permute-start(f32[5,16,8,128]{3,2,1,0:T(8,128)S(1)} %pad_maximum_fusion), channel_id=1, source_target_pairs={{0,0},{1,4},{2,6},{3,2},{4,1},{5,5},{6,7},{7,3},{8,8},{9,12},{10,1... | collective-permute-start | bytes 983048 | tf_op jit(solution)/shard_map/ppermute | solution.py:274
  17.6 22.9 %collective-permute-start.7 = (f32[5,8,32,128]{3,2,1,0:T(8,128)S(1)}, f32[5,8,32,128]{3,2,1,0:T(8,128)S(1)}, u32[]{:S(2)}, u32[]{:S(2)}) collective-permute-start(f32[5,8,32,128]{3,2,1,0:T(8,128)S(1)} %collective-permute-done.3.refs_1_), channel_id=1, source_target_pairs={{1,0},{5,4},{7,6},{3,2},{8,1},{12,5},{14,7},{10,3},{9,8},{13,12},{... | collective-permute-start | bytes 1966088 | tf_op jit(solution)/shard_map/ppermute | solution.py:274
  28.3 10.0 %collective-permute-start.6 = (f32[5,16,8,128]{3,2,1,0:T(8,128)}, f32[5,16,8,128]{3,2,1,0:T(8,128)S(1)}, u32[]{:S(2)}, u32[]{:S(2)}) collective-permute-start(f32[5,16,8,128]{3,2,1,0:T(8,128)} %collective-permute-done.2.refs_0_), channel_id=1, source_target_pairs={{1,0},{5,4},{7,6},{3,2},{8,1},{12,5},{14,7},{10,3},{9,8},{13,12},{... | collective-permute-start | bytes 983048 | tf_op jit(solution)/shard_map/ppermute | solution.py:274
  31.0 9.5 %collective-permute-start.8 = (f32[5,4,32,128]{3,2,1,0:T(8,128)}, f32[5,4,32,128]{3,2,1,0:T(8,128)}, u32[]{:S(2)}, u32[]{:S(2)}) collective-permute-start(f32[5,4,32,128]{3,2,1,0:T(8,128)} %slice.128), channel_id=1, source_target_pairs={{1,0},{5,4},{7,6},{3,2},{8,1},{12,5},{14,7},{10,3},{9,8},{13,12},{... | collective-permute-start | bytes 983048 | tf_op jit(solution)/shard_map/ppermute | solution.py:274
  46.5 6.0 %collective-permute-start.10 = (f32[5,16,4,128]{3,2,1,0:T(4,128)S(1)}, f32[5,16,4,128]{3,2,1,0:T(4,128)S(1)}, u32[]{:S(2)}, u32[]{:S(2)}) collective-permute-start(f32[5,16,4,128]{3,2,1,0:T(4,128)S(1)} %pad_maximum_fusion.8), channel_id=1, source_target_pairs={{4,0},{6,4},{2,6},{0,2},{5,1},{7,5},{3,7},{1,3},{12,8},{14,12},{10... | collective-permute-start | bytes 491528 | tf_op jit(solution)/shard_map/ppermute | solution.py:283
  47.1 16.9 %collective-permute-start.12 = (f32[5,4,32,128]{3,2,1,0:T(8,128)S(1)}, f32[5,4,32,128]{3,2,1,0:T(8,128)S(1)}, u32[]{:S(2)}, u32[]{:S(2)}) collective-permute-start(f32[5,4,32,128]{3,2,1,0:T(8,128)S(1)} %get-tuple-element.26), channel_id=1, source_target_pairs={{1,0},{5,4},{7,6},{3,2},{8,1},{12,5},{14,7},{10,3},{9,8},{13,12},{... | collective-permute-start | bytes 983048 | tf_op jit(solution)/shard_map/ppermute | solution.py:274
  49.0 16.3 %collective-permute-start.13 = (f32[5,8,32,128]{3,2,1,0:T(8,128)S(1)}, f32[5,8,32,128]{3,2,1,0:T(8,128)S(1)}, u32[]{:S(2)}, u32[]{:S(2)}) collective-permute-start(f32[5,8,32,128]{3,2,1,0:T(8,128)S(1)} %get-tuple-element.28.refs_1_), channel_id=1, source_target_pairs={{1,0},{5,4},{7,6},{3,2},{8,1},{12,5},{14,7},{10,3},{9,8},{13,12},{... | collective-permute-start | bytes 1966088 | tf_op jit(solution)/shard_map/ppermute | solution.py:274
  51.5 5.8 %collective-permute-start.9 = (f32[5,16,4,128]{3,2,1,0:T(4,128)S(1)}, f32[5,16,4,128]{3,2,1,0:T(4,128)S(1)}, u32[]{:S(2)}, u32[]{:S(2)}) collective-permute-start(f32[5,16,4,128]{3,2,1,0:T(4,128)S(1)} %pad_maximum_fusion.7), channel_id=1, source_target_pairs={{0,4},{4,6},{6,2},{2,0},{1,5},{5,7},{7,3},{3,1},{8,12},{12,14},{14... | collective-permute-start | bytes 491528 | tf_op jit(solution)/shard_map/ppermute | solution.py:282
  57.4 7.9 %collective-permute-start.11 = (f32[5,12,8,128]{3,2,1,0:T(8,128)S(1)}, f32[5,12,8,128]{3,2,1,0:T(8,128)S(1)}, u32[]{:S(2)}, u32[]{:S(2)}) collective-permute-start(f32[5,12,8,128]{3,2,1,0:T(8,128)S(1)} %pad_maximum_fusion.2), channel_id=1, source_target_pairs={{1,0},{5,4},{7,6},{3,2},{8,1},{12,5},{14,7},{10,3},{9,8},{13,12},{... | collective-permute-start | bytes 737288 | tf_op jit(solution)/shard_map/ppermute | solution.py:274
  70.8 6.0 %collective-permute-start.15 = (f32[5,16,4,128]{3,2,1,0:T(4,128)S(1)}, f32[5,16,4,128]{3,2,1,0:T(4,128)S(1)}, u32[]{:S(2)}, u32[]{:S(2)}) collective-permute-start(f32[5,16,4,128]{3,2,1,0:T(4,128)S(1)} %pad_maximum_fusion.10), channel_id=1, source_target_pairs={{4,0},{6,4},{2,6},{0,2},{5,1},{7,5},{3,7},{1,3},{12,8},{14,12},{10... | collective-permute-start | bytes 491528 | tf_op jit(solution)/shard_map/ppermute | solution.py:283
  72.1 17.0 %collective-permute-start.17 = (f32[5,4,32,128]{3,2,1,0:T(8,128)S(1)}, f32[5,4,32,128]{3,2,1,0:T(8,128)S(1)}, u32[]{:S(2)}, u32[]{:S(2)}) collective-permute-start(f32[5,4,32,128]{3,2,1,0:T(8,128)S(1)} %get-tuple-element.30), channel_id=1, source_target_pairs={{1,0},{5,4},{7,6},{3,2},{8,1},{12,5},{14,7},{10,3},{9,8},{13,12},{... | collective-permute-start | bytes 983048 | tf_op jit(solution)/shard_map/ppermute | solution.py:274
  74.0 16.3 %collective-permute-start.18 = (f32[5,8,32,128]{3,2,1,0:T(8,128)S(1)}, f32[5,8,32,128]{3,2,1,0:T(8,128)S(1)}, u32[]{:S(2)}, u32[]{:S(2)}) collective-permute-start(f32[5,8,32,128]{3,2,1,0:T(8,128)S(1)} %get-tuple-element.32.refs_1_), channel_id=1, source_target_pairs={{1,0},{5,4},{7,6},{3,2},{8,1},{12,5},{14,7},{10,3},{9,8},{13,12},{... | collective-permute-start | bytes 1966088 | tf_op jit(solution)/shard_map/ppermute | solution.py:274
  76.5 5.8 %collective-permute-start.14 = (f32[5,16,4,128]{3,2,1,0:T(4,128)S(1)}, f32[5,16,4,128]{3,2,1,0:T(4,128)S(1)}, u32[]{:S(2)}, u32[]{:S(2)}) collective-permute-start(f32[5,16,4,128]{3,2,1,0:T(4,128)S(1)} %pad_maximum_fusion.9), channel_id=1, source_target_pairs={{0,4},{4,6},{6,2},{2,0},{1,5},{5,7},{7,3},{3,1},{8,12},{12,14},{14... | collective-permute-start | bytes 491528 | tf_op jit(solution)/shard_map/ppermute | solution.py:282
  82.4 7.9 %collective-permute-start.16 = (f32[5,12,8,128]{3,2,1,0:T(8,128)S(1)}, f32[5,12,8,128]{3,2,1,0:T(8,128)S(1)}, u32[]{:S(2)}, u32[]{:S(2)}) collective-permute-start(f32[5,12,8,128]{3,2,1,0:T(8,128)S(1)} %pad_maximum_fusion.4), channel_id=1, source_target_pairs={{1,0},{5,4},{7,6},{3,2},{8,1},{12,5},{14,7},{10,3},{9,8},{13,12},{... | collective-permute-start | bytes 737288 | tf_op jit(solution)/shard_map/ppermute | solution.py:274
  95.8 5.9 %collective-permute-start.20 = (f32[5,16,4,128]{3,2,1,0:T(4,128)S(1)}, f32[5,16,4,128]{3,2,1,0:T(4,128)S(1)}, u32[]{:S(2)}, u32[]{:S(2)}) collective-permute-start(f32[5,16,4,128]{3,2,1,0:T(4,128)S(1)} %pad_maximum_fusion.12), channel_id=1, source_target_pairs={{4,0},{6,4},{2,6},{0,2},{5,1},{7,5},{3,7},{1,3},{12,8},{14,12},{10... | collective-permute-start | bytes 491528 | tf_op jit(solution)/shard_map/ppermute | solution.py:283
  96.0 16.8 %collective-permute-start.23 = (f32[5,4,32,128]{3,2,1,0:T(8,128)S(1)}, f32[5,4,32,128]{3,2,1,0:T(8,128)S(1)}, u32[]{:S(2)}, u32[]{:S(2)}) collective-permute-start(f32[5,4,32,128]{3,2,1,0:T(8,128)S(1)} %get-tuple-element.34), channel_id=1, source_target_pairs={{1,0},{5,4},{7,6},{3,2},{8,1},{12,5},{14,7},{10,3},{9,8},{13,12},{... | collective-permute-start | bytes 983048 | tf_op jit(solution)/shard_map/ppermute | solution.py:274
  97.9 16.3 %collective-permute-start.24 = (f32[5,8,32,128]{3,2,1,0:T(8,128)S(1)}, f32[5,8,32,128]{3,2,1,0:T(8,128)S(1)}, u32[]{:S(2)}, u32[]{:S(2)}) collective-permute-start(f32[5,8,32,128]{3,2,1,0:T(8,128)S(1)} %get-tuple-element.36.refs_1_), channel_id=1, source_target_pairs={{1,0},{5,4},{7,6},{3,2},{8,1},{12,5},{14,7},{10,3},{9,8},{13,12},{... | collective-permute-start | bytes 1966088 | tf_op jit(solution)/shard_map/ppermute | solution.py:274
  100.3 5.8 %collective-permute-start.19 = (f32[5,16,4,128]{3,2,1,0:T(4,128)S(1)}, f32[5,16,4,128]{3,2,1,0:T(4,128)S(1)}, u32[]{:S(2)}, u32[]{:S(2)}) collective-permute-start(f32[5,16,4,128]{3,2,1,0:T(4,128)S(1)} %pad_maximum_fusion.11), channel_id=1, source_target_pairs={{0,4},{4,6},{6,2},{2,0},{1,5},{5,7},{7,3},{3,1},{8,12},{12,14},{14... | collective-permute-start | bytes 491528 | tf_op jit(solution)/shard_map/ppermute | solution.py:282
  106.2 7.9 %collective-permute-start.22 = (f32[5,12,8,128]{3,2,1,0:T(8,128)S(1)}, f32[5,12,8,128]{3,2,1,0:T(8,128)S(1)}, u32[]{:S(2)}, u32[]{:S(2)}) collective-permute-start(f32[5,12,8,128]{3,2,1,0:T(8,128)S(1)} %pad_maximum_fusion.6), channel_id=1, source_target_pairs={{1,0},{5,4},{7,6},{3,2},{8,1},{12,5},{14,7},{10,3},{9,8},{13,12},{... | collective-permute-start | bytes 737288 | tf_op jit(solution)/shard_map/ppermute | solution.py:274
  117.4 18.9 %collective-permute-start.25 = (f32[5,6,32,128]{3,2,1,0:T(8,128)S(1)}, f32[5,6,32,128]{3,2,1,0:T(8,128)S(1)}, u32[]{:S(2)}, u32[]{:S(2)}) collective-permute-start(f32[5,6,32,128]{3,2,1,0:T(8,128)S(1)} %get-tuple-element.40), channel_id=1, source_target_pairs={{0,0},{4,1},{6,2},{2,3},{1,4},{5,5},{7,6},{3,7},{8,8},{12,9},{14,1... | collective-permute-start | bytes 1474568 | tf_op jit(solution)/shard_map/ppermute | solution.py:274
  122.6 13.8 %collective-permute-start.26 = (f32[5,6,32,128]{3,2,1,0:T(8,128)S(1)}, f32[5,6,32,128]{3,2,1,0:T(8,128)S(1)}, u32[]{:S(2)}, u32[]{:S(2)}) collective-permute-start(f32[5,6,32,128]{3,2,1,0:T(8,128)S(1)} %part.17), channel_id=1, source_target_pairs={{0,0},{4,1},{6,2},{2,3},{1,4},{5,5},{7,6},{3,7},{8,8},{12,9},{14,1... | collective-permute-start | bytes 1474568 | tf_op jit(solution)/shard_map/ppermute | solution.py:274
  126.2 10.1 %collective-permute-start.21 = (f32[5,4,32,128]{3,2,1,0:T(8,128)S(1)}, f32[5,4,32,128]{3,2,1,0:T(8,128)S(1)}, u32[]{:S(2)}, u32[]{:S(2)}) collective-permute-start(f32[5,4,32,128]{3,2,1,0:T(8,128)S(1)} %get-tuple-element.38), channel_id=1, source_target_pairs={{0,0},{4,1},{6,2},{2,3},{1,4},{5,5},{7,6},{3,7},{8,8},{12,9},{14,1... | collective-permute-start | bytes 983048 | tf_op jit(solution)/shard_map/ppermute | solution.py:274
  (1 other events, 10.5 us)
where the time goes:
time: 140 us; the launch traced here: 138 us
  starting transfers between devices  50.9 us (36%)
  Pallas kernels  43 us (31%)
  waiting for transfers between devices  38.8 us (28%)
  local copies, waits for them, and re-layouts  2.01 us (1%)
  between operations  1.86 us (1%)
  other arithmetic  1.56 us (1%)
    ppermute x18, starting transfers between devices, moved(): return lax.ppermute(array, AXES, route)  43.6 us
    pallas_call x9, Pallas kernels, part(): pl.pallas_call(functools.partial(part_kernel, turn, away_place, (ng, bloc...  38.3 us
    ppermute x18, waiting for transfers between devices, moved(): return lax.ppermute(array, AXES, route)  24.1 us
    ppermute x4, waiting for transfers between devices, beside(): lax.ppermute(final, AXES, [(where(g, l), where(g, (l + 1) % nl)) for g, l...  14.7 us
    ppermute x4, starting transfers between devices, beside(): lax.ppermute(final, AXES, [(where(g, l), where(g, (l + 1) % nl)) for g, l...  3.79 us
    pallas_call x1, Pallas kernels, on_device(): pl.pallas_call(prepare_kernel, out_shape=[piece(highs), piece(block - hig...  2.96 us
    ppermute x4, starting transfers between devices, beside(): lax.ppermute(first, AXES, [(where(g, (l + 1) % nl), where(g, l)) for g, l...  2.81 us
  transfers between devices with their start and end apart: 27, of which 10 were waited for; matrix products, arithmetic and copies ran while one was open for 2% of the time, Pallas kernels for 13%

commit v1 on v0

--- a/solution.py
+++ b/solution.py
@@ -210,38 +210,32 @@
                 put(at - SHIFT + j, here, melt(table, index[turn, j, here]))
 
 
-def prepare_kernel(labels_in, roughness_in, potential_in, *refs):
-    outs, (first_rows, final_rows), (labels, roughness, potential, sems) = refs[:-6], refs[-6:-4], refs[-4:]
-    rows = labels.shape[1]
-    starts = (0, outs[0].shape[1])
-    ranges = [(ref, at, at + ref.shape[1]) for ref, at in zip(outs, starts)]
-    marks = sorted(set(m for _, *ends in ranges for m in ends))
-    copies = []
-    for n, (first, stop) in enumerate(zip(marks, marks[1:])):
-        span = pl.ds(first, stop - first)
-        pairs = [(labels_in.at[span], labels.at[span])]
-        pairs += [(roughness_in.at[a, span], roughness.at[a, span]) for a in range(4)]
-        pairs += [(potential_in.at[k, span], potential.at[k, span]) for k in range(2)]
-        copies.append([pltpu.make_async_copy(*pair, sems.at[n, i]) for i, pair in enumerate(pairs)])
-        for copy in copies[-1]:
-            copy.start()
-    for n, (first, stop) in enumerate(zip(marks, marks[1:])):
-        targets = [(ref, at) for ref, at, until in ranges if at <= first and stop <= until]
-        for copy in copies[n]:
-            copy.wait()
-
-        @pl.loop(first, stop)
-        def _(o, targets=targets):
-            kind = labels[o]
-            rough = [roughness[a, o] for a in range(4)]
-            inverse = 1.0 / (3.0 + rough[0] + rough[1] + rough[2] + rough[3])
-            new = [(jnp.where(kind == a, 3.0, 0.0) + rough[a]) * inverse for a in range(3)]
-            new += [potential[0, o], potential[1, o]]
-            for f, value in enumerate(new):
-                for ref, at in targets:
-                    ref[f, o - at] = value
-                first_rows[f, o] = value[:STEPS]
-                final_rows[f, o] = value[rows - STEPS :]
+def prepare_kernel(first, labels_in, roughness_in, potential_in, *refs):
+    before, (state, first_rows, final_rows), (labels, roughness, potential, sems) = refs[:-7], refs[-7:-4], refs[-4:]
+    planes, rows = labels.shape[:2]
+    span = pl.ds(first, planes)
+    pairs = [(labels_in.at[span], labels)]
+    pairs += [(roughness_in.at[a, span], roughness.at[a]) for a in range(4)]
+    pairs += [(potential_in.at[k, span], potential.at[k]) for k in range(2)]
+    copies = [pltpu.make_async_copy(*pair, sems.at[i]) for i, pair in enumerate(pairs)]
+    for copy in copies:
+        copy.start()
+    for old, new in zip(before, (first_rows, final_rows)):
+        new[:, :first] = old[...]
+    for copy in copies:
+        copy.wait()
+
+    @pl.loop(0, planes)
+    def _(o):
+        kind = labels[o]
+        rough = [roughness[a, o] for a in range(4)]
+        inverse = 1.0 / (3.0 + rough[0] + rough[1] + rough[2] + rough[3])
+        new = [(jnp.where(kind == a, 3.0, 0.0) + rough[a]) * inverse for a in range(3)]
+        new += [potential[0, o], potential[1, o]]
+        for f, value in enumerate(new):
+            state[f, o] = value
+            first_rows[f, o + first] = value[:STEPS]
+            final_rows[f, o + first] = value[rows - STEPS :]
 
 
 def on_device(ng, nl, labels, roughness, potential, grad_coef, composition, latent, diffusivity, melt_table, melt_index):
@@ -319,24 +313,26 @@
             name="part",
         )(table, *args)
 
-    away_index = lax.ppermute(
-        melt_index, AXES, [(away(ng - 1, l) // nl * nl + l, away(ng - 1, l)) for l in range(nl)]
-    )
-
-    front, back, first_rows, final_rows = pl.pallas_call(
-        prepare_kernel,
-        out_shape=[piece(highs), piece(block - highs)] + [piece(block, STEPS)] * 2,
-        in_specs=[pl.BlockSpec(memory_space=pltpu.HBM)] * 3,
-        out_specs=[vmem] * 4,
-        scratch_shapes=[
-            pltpu.VMEM(labels.shape, jnp.int32),
-            pltpu.VMEM(roughness.shape, f32),
-            pltpu.VMEM(potential.shape, f32),
-            pltpu.SemaphoreType.DMA((2, 7)),
-        ],
-        compiler_params=limit(58),
-        name="prepare",
-    )(labels, roughness, potential)
+    away_index = lax.ppermute(melt_index, AXES, [(away(ng - 1, l) // nl * nl + l, away(ng - 1, l)) for l in range(nl)])
+
+    def prepare(first, planes, *before):
+        return pl.pallas_call(
+            functools.partial(prepare_kernel, first),
+            out_shape=[piece(planes)] + [piece(first + planes, STEPS)] * 2,
+            in_specs=[pl.BlockSpec(memory_space=pltpu.HBM)] * 3 + [vmem] * len(before),
+            out_specs=[vmem] * 3,
+            scratch_shapes=[
+                pltpu.VMEM((planes, rows, lanes), jnp.int32),
+                pltpu.VMEM((4, planes, rows, lanes), f32),
+                pltpu.VMEM((2, planes, rows, lanes), f32),
+                pltpu.SemaphoreType.DMA((7,)),
+            ],
+            compiler_params=limit(58),
+            name="prepare",
+        )(labels, roughness, potential, *before)
+
+    front, *edge_rows = prepare(0, highs)
+    back, first_rows, final_rows = prepare(highs, block - highs, *edge_rows)
 
     def packed(left, right, first, stop):
         return jnp.concatenate([left[:, first:stop], right[:, first:stop]], axis=2)
@@ -405,17 +401,7 @@
 
     cut = 2
     middle, seam = part(
-        turn,
-        kept,
-        [(lows, 0, 0), (cut, lows, 0)],
-        True,
-        True,
-        [(lows, lows + cut)],
-        False,
-        seam,
-        halo,
-        low,
-        above,
+        turn, kept, [(lows, 0, 0), (cut, lows, 0)], True, True, [(lows, lows + cut)], False, seam, halo, low, above
     )
     middle = moved(middle, away, home, 0)
     (final,) = part(

time: 140 us -> 142 us (1.014)
  Pallas kernels: 43 us -> 45.7 us
    pallas_call x1 -> x2, Pallas kernels: 2.96 us -> 5.65 us  [prepare(): pl.pallas_call(functools.partial(prepare_kernel, first), out_shape=[piece...]
where the time goes in v1:
time: 142 us; the launch traced here: 141 us
  starting transfers between devices  50.9 us (36%)
  Pallas kernels  45.7 us (32%)
  waiting for transfers between devices  38.8 us (27%)
  local copies, waits for them, and re-layouts  2.02 us (1%)
  between operations  1.86 us (1%)
  other arithmetic  1.56 us (1%)
    ppermute x18, starting transfers between devices, moved(): return lax.ppermute(array, AXES, route)  43.6 us
    pallas_call x9, Pallas kernels, part(): pl.pallas_call(functools.partial(part_kernel, turn, away_place, (ng, bloc...  38.3 us
    ppermute x18, waiting for transfers between devices, moved(): return lax.ppermute(array, AXES, route)  24.1 us
    ppermute x4, waiting for transfers between devices, beside(): lax.ppermute(final, AXES, [(where(g, l), where(g, (l + 1) % nl)) for g, l...  14.7 us
    pallas_call x2, Pallas kernels, prepare(): pl.pallas_call(functools.partial(prepare_kernel, first), out_shape=[piece...  5.65 us
    ppermute x4, starting transfers between devices, beside(): lax.ppermute(final, AXES, [(where(g, l), where(g, (l + 1) % nl)) for g, l...  3.79 us
  transfers between devices with their start and end apart: 27, of which 10 were waited for; matrix products, arithmetic and copies ran while one was open for 2% of the time, Pallas kernels for 13%

profile of v1, /device:TPU:17, one launch (start us, length us, event | category | flops | bytes accessed | tf_op | source)
XLA Modules:
  0.0 140.9 jit_solution(18187283737711124271)
XLA Ops:
  0.6 2.3 %prepare.2 = (f32[5,8,32,128]{3,2,1,0:T(8,128)}, f32[5,8,4,128]{3,2,1,0:T(4,128)}, f32[5,8,4,128]{3,2,1,0:T(4,128)}) custom-call(s32[16,32,128]{2,1,0:T(8,128)} %labels_in.3, f32[4,16,32,128]{3,2,1,0:T(8,128)} %roughness_in.3, f32[2,16,32,128]{3,2,1,0:T(8,128)} %potential_in.3), custom_call_target="tpu_custom_call" | custom-call | tf_op jit(solution)/shard_map/prepare/pallas_call | solution.py:319
  3.0 3.3 %prepare.3 = (f32[5,8,32,128]{3,2,1,0:T(8,128)}, f32[5,16,4,128]{3,2,1,0:T(4,128)}, f32[5,16,4,128]{3,2,1,0:T(4,128)}) custom-call(s32[16,32,128]{2,1,0:T(8,128)} %labels_in.3, f32[4,16,32,128]{3,2,1,0:T(8,128)} %roughness_in.3, f32[2,16,32,128]{3,2,1,0:T(8,128)} %potential_in.3, f32[5,8,4,128]{3,2,1,0:T(4,128)} %get-tuple-element.24.refs_0_, ...), custom_call_target="tpu_custom_call" | custom-call | tf_op jit(solution)/shard_map/prepare/pallas_call | solution.py:319
  8.3 2.8 %collective-permute-start.3 = (f32[5,8,32,128]{3,2,1,0:T(8,128)}, f32[5,8,32,128]{3,2,1,0:T(8,128)S(1)}, u32[]{:S(2)}, u32[]{:S(2)}) collective-permute-start(f32[5,8,32,128]{3,2,1,0:T(8,128)} %get-tuple-element.28), channel_id=1, source_target_pairs={{0,0},{1,4},{2,6},{3,2},{4,1},{5,5},{6,7},{7,3},{8,8},{9,12},{10,1... | collective-permute-start | bytes 1966088 | tf_op jit(solution)/shard_map/ppermute | solution.py:268
  11.1 2.8 %collective-permute-start.4 = (f32[5,8,32,128]{3,2,1,0:T(8,128)}, f32[5,8,32,128]{3,2,1,0:T(8,128)S(1)}, u32[]{:S(2)}, u32[]{:S(2)}) collective-permute-start(f32[5,8,32,128]{3,2,1,0:T(8,128)} %get-tuple-element.29), channel_id=1, source_target_pairs={{0,0},{1,4},{2,6},{3,2},{4,1},{5,5},{6,7},{7,3},{8,8},{9,12},{10,1... | collective-permute-start | bytes 1966088 | tf_op jit(solution)/shard_map/ppermute | solution.py:268
  15.1 2.8 %collective-permute-start.2 = (f32[5,16,8,128]{3,2,1,0:T(8,128)S(1)}, f32[5,16,8,128]{3,2,1,0:T(8,128)}, u32[]{:S(2)}, u32[]{:S(2)}) collective-permute-start(f32[5,16,8,128]{3,2,1,0:T(8,128)S(1)} %pad_maximum_fusion), channel_id=1, source_target_pairs={{0,0},{1,4},{2,6},{3,2},{4,1},{5,5},{6,7},{7,3},{8,8},{9,12},{10,1... | collective-permute-start | bytes 983048 | tf_op jit(solution)/shard_map/ppermute | solution.py:268
  20.4 1.9 %collective-permute-start.7 = (f32[5,8,32,128]{3,2,1,0:T(8,128)S(1)}, f32[5,8,32,128]{3,2,1,0:T(8,128)S(1)}, u32[]{:S(2)}, u32[]{:S(2)}) collective-permute-start(f32[5,8,32,128]{3,2,1,0:T(8,128)S(1)} %collective-permute-done.3.refs_1_), channel_id=1, source_target_pairs={{1,0},{5,4},{7,6},{3,2},{8,1},{12,5},{14,7},{10,3},{9,8},{13,12},{... | collective-permute-start | bytes 1966088 | tf_op jit(solution)/shard_map/ppermute | solution.py:268
  22.3 8.7 %collective-permute-done.2.refs_0_ = f32[5,16,8,128]{3,2,1,0:T(8,128)} collective-permute-done((f32[5,16,8,128]{3,2,1,0:T(8,128)S(1)}, f32[5,16,8,128]{3,2,1,0:T(8,128)}, u32[]{:S(2)}, u32[]{:S(2)}) %collective-permute-start.2) | collective-permute-done | bytes 327712 | tf_op jit(solution)/shard_map/ppermute | solution.py:268
  31.0 1.9 %collective-permute-start.6 = (f32[5,16,8,128]{3,2,1,0:T(8,128)}, f32[5,16,8,128]{3,2,1,0:T(8,128)S(1)}, u32[]{:S(2)}, u32[]{:S(2)}) collective-permute-start(f32[5,16,8,128]{3,2,1,0:T(8,128)} %collective-permute-done.2.refs_0_), channel_id=1, source_target_pairs={{1,0},{5,4},{7,6},{3,2},{8,1},{12,5},{14,7},{10,3},{9,8},{13,12},{... | collective-permute-start | bytes 983048 | tf_op jit(solution)/shard_map/ppermute | solution.py:268
  33.7 2.4 %collective-permute-start.8 = (f32[5,4,32,128]{3,2,1,0:T(8,128)}, f32[5,4,32,128]{3,2,1,0:T(8,128)}, u32[]{:S(2)}, u32[]{:S(2)}) collective-permute-start(f32[5,4,32,128]{3,2,1,0:T(8,128)} %slice.128), channel_id=1, source_target_pairs={{1,0},{5,4},{7,6},{3,2},{8,1},{12,5},{14,7},{10,3},{9,8},{13,12},{... | collective-permute-start | bytes 983048 | tf_op jit(solution)/shard_map/ppermute | solution.py:268
  36.9 4.1 %part.9 = (f32[5,4,32,128]{3,2,1,0:T(8,128)S(1)}, f32[4,6,2,48,128]{4,3,2,1,0:T(8,128)S(1)}) custom-call(f32[72]{0:T(128)S(1)} %concatenate.42.table, f32[5,16,8,128]{3,2,1,0:T(8,128)} %collective-permute-done.2.refs_0_, f32[5,8,32,128]{3,2,1,0:T(8,128)S(1)} %collective-permute-done.3.refs_1_, f32[5,8,32,128]{3,2,1,0:T(8,128)S(1)} %collective-permute-done.4.refs_2_), custom_call_target="tpu_custom_call" | custom-call | flops 153354240 | bytes 4000000 | tf_op jit(solution)/shard_map/part/pallas_call | solution.py:294
  41.0 2.2 %collective-permute-done.8.refs_4_ = f32[5,4,32,128]{3,2,1,0:T(8,128)} collective-permute-done((f32[5,4,32,128]{3,2,1,0:T(8,128)}, f32[5,4,32,128]{3,2,1,0:T(8,128)}, u32[]{:S(2)}, u32[]{:S(2)}) %collective-permute-start.8) | collective-permute-done | bytes 327712 | tf_op jit(solution)/shard_map/ppermute | solution.py:268
  43.2 5.8 %part.10 = (f32[5,8,32,128]{3,2,1,0:T(8,128)S(1)}, f32[5,4,32,128]{3,2,1,0:T(8,128)S(1)}) custom-call(f32[72]{0:T(128)S(1)} %concatenate.42.table, f32[4,6,2,48,128]{4,3,2,1,0:T(8,128)S(1)} %get-tuple-element.31.refs_0_, s32[4,8,32,128]{3,2,1,0:T(8,128)S(1)} %collective-permute-done.5.refs_1_, f32[5,16,8,128]{3,2,1,0:T(8,128)S(1)} %collective-permute-done.6.refs_2_, ...), custom_call_target="tpu_custom_call" | custom-call | flops 153354240 | bytes 4000000 | tf_op jit(solution)/shard_map/part/pallas_call | solution.py:294
  51.7 2.5 %collective-permute-start.13 = (f32[5,8,32,128]{3,2,1,0:T(8,128)S(1)}, f32[5,8,32,128]{3,2,1,0:T(8,128)S(1)}, u32[]{:S(2)}, u32[]{:S(2)}) collective-permute-start(f32[5,8,32,128]{3,2,1,0:T(8,128)S(1)} %get-tuple-element.32.refs_1_), channel_id=1, source_target_pairs={{1,0},{5,4},{7,6},{3,2},{8,1},{12,5},{14,7},{10,3},{9,8},{13,12},{... | collective-permute-start | bytes 1966088 | tf_op jit(solution)/shard_map/ppermute | solution.py:268
  55.2 4.8 %collective-permute-done.9 = f32[5,16,4,128]{3,2,1,0:T(4,128)S(1)} collective-permute-done((f32[5,16,4,128]{3,2,1,0:T(4,128)S(1)}, f32[5,16,4,128]{3,2,1,0:T(4,128)S(1)}, u32[]{:S(2)}, u32[]{:S(2)}) %collective-permute-start.9) | collective-permute-done | bytes 163872 | tf_op jit(solution)/shard_map/ppermute | solution.py:276
  60.1 2.8 %collective-permute-start.11 = (f32[5,12,8,128]{3,2,1,0:T(8,128)S(1)}, f32[5,12,8,128]{3,2,1,0:T(8,128)S(1)}, u32[]{:S(2)}, u32[]{:S(2)}) collective-permute-start(f32[5,12,8,128]{3,2,1,0:T(8,128)S(1)} %pad_maximum_fusion.2), channel_id=1, source_target_pairs={{1,0},{5,4},{7,6},{3,2},{8,1},{12,5},{14,7},{10,3},{9,8},{13,12},{... | collective-permute-start | bytes 737288 | tf_op jit(solution)/shard_map/ppermute | solution.py:268
  62.9 3.7 %part.11 = (f32[5,4,32,128]{3,2,1,0:T(8,128)S(1)}, f32[4,6,2,48,128]{4,3,2,1,0:T(8,128)S(1)}) custom-call(f32[72]{0:T(128)S(1)} %concatenate.42.table, f32[5,12,8,128]{3,2,1,0:T(8,128)S(1)} %pad_maximum_fusion.1.refs_0_, f32[5,8,32,128]{3,2,1,0:T(8,128)S(1)} %get-tuple-element.32.refs_1_, f32[5,4,32,128]{3,2,1,0:T(8,128)S(1)} %get-tuple-element.33.refs_2_), custom_call_target="tpu_custom_call" | custom-call | flops 153354240 | bytes 4000000 | tf_op jit(solution)/shard_map/part/pallas_call | solution.py:294
  68.0 5.4 %part.12 = (f32[5,8,32,128]{3,2,1,0:T(8,128)S(1)}, f32[5,4,32,128]{3,2,1,0:T(8,128)S(1)}) custom-call(f32[72]{0:T(128)S(1)} %concatenate.42.table, f32[4,6,2,48,128]{4,3,2,1,0:T(8,128)S(1)} %get-tuple-element.35.refs_0_, s32[4,8,32,128]{3,2,1,0:T(8,128)S(1)} %collective-permute-done.5.refs_1_, f32[5,12,8,128]{3,2,1,0:T(8,128)S(1)} %collective-permute-done.11.refs_2_, ...), custom_call_target="tpu_custom_call" | custom-call | flops 153354240 | bytes 4000000 | tf_op jit(solution)/shard_map/part/pallas_call | solution.py:294
  76.7 2.4 %collective-permute-start.18 = (f32[5,8,32,128]{3,2,1,0:T(8,128)S(1)}, f32[5,8,32,128]{3,2,1,0:T(8,128)S(1)}, u32[]{:S(2)}, u32[]{:S(2)}) collective-permute-start(f32[5,8,32,128]{3,2,1,0:T(8,128)S(1)} %get-tuple-element.36.refs_1_), channel_id=1, source_target_pairs={{1,0},{5,4},{7,6},{3,2},{8,1},{12,5},{14,7},{10,3},{9,8},{13,12},{... | collective-permute-start | bytes 1966088 | tf_op jit(solution)/shard_map/ppermute | solution.py:268
  79.5 5.5 %collective-permute-done.14 = f32[5,16,4,128]{3,2,1,0:T(4,128)S(1)} collective-permute-done((f32[5,16,4,128]{3,2,1,0:T(4,128)S(1)}, f32[5,16,4,128]{3,2,1,0:T(4,128)S(1)}, u32[]{:S(2)}, u32[]{:S(2)}) %collective-permute-start.14) | collective-permute-done | bytes 163872 | tf_op jit(solution)/shard_map/ppermute | solution.py:276
  85.1 3.0 %collective-permute-start.16 = (f32[5,12,8,128]{3,2,1,0:T(8,128)S(1)}, f32[5,12,8,128]{3,2,1,0:T(8,128)S(1)}, u32[]{:S(2)}, u32[]{:S(2)}) collective-permute-start(f32[5,12,8,128]{3,2,1,0:T(8,128)S(1)} %pad_maximum_fusion.4), channel_id=1, source_target_pairs={{1,0},{5,4},{7,6},{3,2},{8,1},{12,5},{14,7},{10,3},{9,8},{13,12},{... | collective-permute-start | bytes 737288 | tf_op jit(solution)/shard_map/ppermute | solution.py:268
  88.1 3.7 %part.13 = (f32[5,4,32,128]{3,2,1,0:T(8,128)S(1)}, f32[4,6,2,48,128]{4,3,2,1,0:T(8,128)S(1)}) custom-call(f32[72]{0:T(128)S(1)} %concatenate.42.table, f32[5,12,8,128]{3,2,1,0:T(8,128)S(1)} %pad_maximum_fusion.3.refs_0_, f32[5,8,32,128]{3,2,1,0:T(8,128)S(1)} %get-tuple-element.36.refs_1_, f32[5,4,32,128]{3,2,1,0:T(8,128)S(1)} %get-tuple-element.37.refs_2_), custom_call_target="tpu_custom_call" | custom-call | flops 153354240 | bytes 4000000 | tf_op jit(solution)/shard_map/part/pallas_call | solution.py:294
  93.0 5.4 %part.14 = (f32[5,8,32,128]{3,2,1,0:T(8,128)S(1)}, f32[5,4,32,128]{3,2,1,0:T(8,128)S(1)}) custom-call(f32[72]{0:T(128)S(1)} %concatenate.42.table, f32[4,6,2,48,128]{4,3,2,1,0:T(8,128)S(1)} %get-tuple-element.39.refs_0_, s32[4,8,32,128]{3,2,1,0:T(8,128)S(1)} %collective-permute-done.5.refs_1_, f32[5,12,8,128]{3,2,1,0:T(8,128)S(1)} %collective-permute-done.16.refs_2_, ...), custom_call_target="tpu_custom_call" | custom-call | flops 153354240 | bytes 4000000 | tf_op jit(solution)/shard_map/part/pallas_call | solution.py:294
  100.6 2.4 %collective-permute-start.24 = (f32[5,8,32,128]{3,2,1,0:T(8,128)S(1)}, f32[5,8,32,128]{3,2,1,0:T(8,128)S(1)}, u32[]{:S(2)}, u32[]{:S(2)}) collective-permute-start(f32[5,8,32,128]{3,2,1,0:T(8,128)S(1)} %get-tuple-element.40.refs_1_), channel_id=1, source_target_pairs={{1,0},{5,4},{7,6},{3,2},{8,1},{12,5},{14,7},{10,3},{9,8},{13,12},{... | collective-permute-start | bytes 1966088 | tf_op jit(solution)/shard_map/ppermute | solution.py:268
  104.5 4.3 %collective-permute-done.19 = f32[5,16,4,128]{3,2,1,0:T(4,128)S(1)} collective-permute-done((f32[5,16,4,128]{3,2,1,0:T(4,128)S(1)}, f32[5,16,4,128]{3,2,1,0:T(4,128)S(1)}, u32[]{:S(2)}, u32[]{:S(2)}) %collective-permute-start.19) | collective-permute-done | bytes 163872 | tf_op jit(solution)/shard_map/ppermute | solution.py:276
  108.9 2.8 %collective-permute-start.22 = (f32[5,12,8,128]{3,2,1,0:T(8,128)S(1)}, f32[5,12,8,128]{3,2,1,0:T(8,128)S(1)}, u32[]{:S(2)}, u32[]{:S(2)}) collective-permute-start(f32[5,12,8,128]{3,2,1,0:T(8,128)S(1)} %pad_maximum_fusion.6), channel_id=1, source_target_pairs={{1,0},{5,4},{7,6},{3,2},{8,1},{12,5},{14,7},{10,3},{9,8},{13,12},{... | collective-permute-start | bytes 737288 | tf_op jit(solution)/shard_map/ppermute | solution.py:268
  111.8 3.7 %part.15 = (f32[5,4,32,128]{3,2,1,0:T(8,128)S(1)}, f32[4,6,2,48,128]{4,3,2,1,0:T(8,128)S(1)}) custom-call(f32[72]{0:T(128)S(1)} %concatenate.42.table, f32[5,12,8,128]{3,2,1,0:T(8,128)S(1)} %pad_maximum_fusion.5.refs_0_, f32[5,8,32,128]{3,2,1,0:T(8,128)S(1)} %get-tuple-element.40.refs_1_, f32[5,4,32,128]{3,2,1,0:T(8,128)S(1)} %get-tuple-element.41.refs_2_), custom_call_target="tpu_custom_call" | custom-call | flops 153354240 | bytes 4000000 | tf_op jit(solution)/shard_map/part/pallas_call | solution.py:294
  116.9 3.3 %part.16 = (f32[5,6,32,128]{3,2,1,0:T(8,128)S(1)}, f32[4,6,2,48,128]{4,3,2,1,0:T(8,128)S(1)}) custom-call(f32[72]{0:T(128)S(1)} %concatenate.42.table, f32[4,6,2,48,128]{4,3,2,1,0:T(8,128)S(1)} %get-tuple-element.43.refs_0_, f32[5,12,8,128]{3,2,1,0:T(8,128)S(1)} %collective-permute-done.22.refs_1_, f32[5,4,32,128]{3,2,1,0:T(8,128)S(1)} %collective-permute-done.23.refs_2_, ...), custom_call_target="tpu_custom_call" | custom-call | flops 76677120 | bytes 4000000 | tf_op jit(solution)/shard_map/part/pallas_call | solution.py:294
  120.2 1.9 %collective-permute-start.25 = (f32[5,6,32,128]{3,2,1,0:T(8,128)S(1)}, f32[5,6,32,128]{3,2,1,0:T(8,128)S(1)}, u32[]{:S(2)}, u32[]{:S(2)}) collective-permute-start(f32[5,6,32,128]{3,2,1,0:T(8,128)S(1)} %get-tuple-element.44), channel_id=1, source_target_pairs={{0,0},{4,1},{6,2},{2,3},{1,4},{5,5},{7,6},{3,7},{8,8},{12,9},{14,1... | collective-permute-start | bytes 1474568 | tf_op jit(solution)/shard_map/ppermute | solution.py:268
  122.1 3.2 %part.17 = f32[5,6,32,128]{3,2,1,0:T(8,128)S(1)} custom-call(f32[72]{0:T(128)S(1)} %concatenate.42.table, f32[4,6,2,48,128]{4,3,2,1,0:T(8,128)S(1)} %get-tuple-element.45.refs_0_, f32[5,12,8,128]{3,2,1,0:T(8,128)S(1)} %collective-permute-done.22.refs_1_, f32[5,8,32,128]{3,2,1,0:T(8,128)S(1)} %collective-permute-done.24.refs_3_.refs_2_), custom_call_target="tpu_custom_call" | custom-call | flops 76677120 | bytes 4000000 | tf_op jit(solution)/shard_map/part/pallas_call | solution.py:294
  125.3 3.6 %collective-permute-start.26 = (f32[5,6,32,128]{3,2,1,0:T(8,128)S(1)}, f32[5,6,32,128]{3,2,1,0:T(8,128)S(1)}, u32[]{:S(2)}, u32[]{:S(2)}) collective-permute-start(f32[5,6,32,128]{3,2,1,0:T(8,128)S(1)} %part.17), channel_id=1, source_target_pairs={{0,0},{4,1},{6,2},{2,3},{1,4},{5,5},{7,6},{3,7},{8,8},{12,9},{14,1... | collective-permute-start | bytes 1474568 | tf_op jit(solution)/shard_map/ppermute | solution.py:268
  128.9 1.9 %collective-permute-start.21 = (f32[5,4,32,128]{3,2,1,0:T(8,128)S(1)}, f32[5,4,32,128]{3,2,1,0:T(8,128)S(1)}, u32[]{:S(2)}, u32[]{:S(2)}) collective-permute-start(f32[5,4,32,128]{3,2,1,0:T(8,128)S(1)} %get-tuple-element.42), channel_id=1, source_target_pairs={{0,0},{4,1},{6,2},{2,3},{1,4},{5,5},{7,6},{3,7},{8,8},{12,9},{14,1... | collective-permute-start | bytes 983048 | tf_op jit(solution)/shard_map/ppermute | solution.py:268
  130.9 8.2 %collective-permute-done.21.refs_0_ = f32[5,4,32,128]{3,2,1,0:T(8,128)S(1)} collective-permute-done((f32[5,4,32,128]{3,2,1,0:T(8,128)S(1)}, f32[5,4,32,128]{3,2,1,0:T(8,128)S(1)}, u32[]{:S(2)}, u32[]{:S(2)}) %collective-permute-start.21) | collective-permute-done | bytes 327712 | tf_op jit(solution)/shard_map/ppermute | solution.py:268
  (91 shorter events, 23.5 us)
Async XLA Ops:
  3.0 11.6 %copy-start.2 = (f32[4,3]{1,0:T(4,128)S(1)}, f32[4,3]{1,0:T(4,128)}, u32[]{:S(2)}) copy-start(f32[4,3]{1,0:T(4,128)} %param.12) | copy-start | bytes 148
  3.0 11.7 %copy-start.1 = (f32[4,2]{0,1:T(2,128)S(1)}, f32[4,2]{0,1:T(2,128)}, u32[]{:S(2)}) copy-start(f32[4,2]{0,1:T(2,128)} %param.13) | copy-start | bytes 100
  3.0 15.0 %copy-start.4 = (f32[4]{0:T(128)S(1)}, f32[4]{0:T(128)}, u32[]{:S(2)}) copy-start(f32[4]{0:T(128)} %param.14) | copy-start | bytes 52
  3.0 33.1 %copy-start.5 = (f32[2]{0:T(128)S(1)}, f32[2]{0:T(128)}, u32[]{:S(2)}) copy-start(f32[2]{0:T(128)} %param.15) | copy-start | bytes 28
  6.4 30.2 %copy-start.3 = (f32[16,2]{0,1:T(2,128)S(1)}, f32[16,2]{0,1:T(2,128)}, u32[]{:S(2)}) copy-start(f32[16,2]{0,1:T(2,128)} %param.16) | copy-start | bytes 388
  6.4 8.6 %collective-permute-start.1 = (f32[5,16,4,128]{3,2,1,0:T(4,128)}, f32[5,16,4,128]{3,2,1,0:T(4,128)S(1)}, u32[]{:S(2)}, u32[]{:S(2)}) collective-permute-start(f32[5,16,4,128]{3,2,1,0:T(4,128)} %get-tuple-element.27), channel_id=1, source_target_pairs={{1,0},{2,1},{3,2},{0,3},{5,4},{6,5},{7,6},{4,7},{9,8},{10,9},{11,1... | collective-permute-start | bytes 491528 | tf_op jit(solution)/shard_map/ppermute | solution.py:277
  7.1 7.9 %collective-permute-start = (f32[5,16,4,128]{3,2,1,0:T(4,128)}, f32[5,16,4,128]{3,2,1,0:T(4,128)S(1)}, u32[]{:S(2)}, u32[]{:S(2)}) collective-permute-start(f32[5,16,4,128]{3,2,1,0:T(4,128)} %get-tuple-element.26), channel_id=1, source_target_pairs={{0,1},{1,2},{2,3},{3,0},{4,5},{5,6},{6,7},{7,4},{8,9},{9,10},{10,1... | collective-permute-start | bytes 491528 | tf_op jit(solution)/shard_map/ppermute | solution.py:276
  8.3 12.1 %collective-permute-start.3 = (f32[5,8,32,128]{3,2,1,0:T(8,128)}, f32[5,8,32,128]{3,2,1,0:T(8,128)S(1)}, u32[]{:S(2)}, u32[]{:S(2)}) collective-permute-start(f32[5,8,32,128]{3,2,1,0:T(8,128)} %get-tuple-element.28), channel_id=1, source_target_pairs={{0,0},{1,4},{2,6},{3,2},{4,1},{5,5},{6,7},{7,3},{8,8},{9,12},{10,1... | collective-permute-start | bytes 1966088 | tf_op jit(solution)/shard_map/ppermute | solution.py:268
  11.1 21.9 %collective-permute-start.4 = (f32[5,8,32,128]{3,2,1,0:T(8,128)}, f32[5,8,32,128]{3,2,1,0:T(8,128)S(1)}, u32[]{:S(2)}, u32[]{:S(2)}) collective-permute-start(f32[5,8,32,128]{3,2,1,0:T(8,128)} %get-tuple-element.29), channel_id=1, source_target_pairs={{0,0},{1,4},{2,6},{3,2},{4,1},{5,5},{6,7},{7,3},{8,8},{9,12},{10,1... | collective-permute-start | bytes 1966088 | tf_op jit(solution)/shard_map/ppermute | solution.py:268
  13.8 27.2 %collective-permute-start.5 = (s32[4,8,32,128]{3,2,1,0:T(8,128)S(1)}, s32[4,8,32,128]{3,2,1,0:T(8,128)S(1)}, u32[]{:S(2)}, u32[]{:S(2)}) collective-permute-start(s32[4,8,32,128]{3,2,1,0:T(8,128)S(1)} %copy-done), channel_id=1, source_target_pairs={{24,25},{29,29},{30,31},{27,27}} | collective-permute-start | bytes 1572872 | tf_op jit(solution)/shard_map/ppermute | solution.py:316
  15.1 15.9 %collective-permute-start.2 = (f32[5,16,8,128]{3,2,1,0:T(8,128)S(1)}, f32[5,16,8,128]{3,2,1,0:T(8,128)}, u32[]{:S(2)}, u32[]{:S(2)}) collective-permute-start(f32[5,16,8,128]{3,2,1,0:T(8,128)S(1)} %pad_maximum_fusion), channel_id=1, source_target_pairs={{0,0},{1,4},{2,6},{3,2},{4,1},{5,5},{6,7},{7,3},{8,8},{9,12},{10,1... | collective-permute-start | bytes 983048 | tf_op jit(solution)/shard_map/ppermute | solution.py:268
  20.4 22.9 %collective-permute-start.7 = (f32[5,8,32,128]{3,2,1,0:T(8,128)S(1)}, f32[5,8,32,128]{3,2,1,0:T(8,128)S(1)}, u32[]{:S(2)}, u32[]{:S(2)}) collective-permute-start(f32[5,8,32,128]{3,2,1,0:T(8,128)S(1)} %collective-permute-done.3.refs_1_), channel_id=1, source_target_pairs={{1,0},{5,4},{7,6},{3,2},{8,1},{12,5},{14,7},{10,3},{9,8},{13,12},{... | collective-permute-start | bytes 1966088 | tf_op jit(solution)/shard_map/ppermute | solution.py:268
  31.0 10.0 %collective-permute-start.6 = (f32[5,16,8,128]{3,2,1,0:T(8,128)}, f32[5,16,8,128]{3,2,1,0:T(8,128)S(1)}, u32[]{:S(2)}, u32[]{:S(2)}) collective-permute-start(f32[5,16,8,128]{3,2,1,0:T(8,128)} %collective-permute-done.2.refs_0_), channel_id=1, source_target_pairs={{1,0},{5,4},{7,6},{3,2},{8,1},{12,5},{14,7},{10,3},{9,8},{13,12},{... | collective-permute-start | bytes 983048 | tf_op jit(solution)/shard_map/ppermute | solution.py:268
  33.7 9.5 %collective-permute-start.8 = (f32[5,4,32,128]{3,2,1,0:T(8,128)}, f32[5,4,32,128]{3,2,1,0:T(8,128)}, u32[]{:S(2)}, u32[]{:S(2)}) collective-permute-start(f32[5,4,32,128]{3,2,1,0:T(8,128)} %slice.128), channel_id=1, source_target_pairs={{1,0},{5,4},{7,6},{3,2},{8,1},{12,5},{14,7},{10,3},{9,8},{13,12},{... | collective-permute-start | bytes 983048 | tf_op jit(solution)/shard_map/ppermute | solution.py:268
  49.2 6.0 %collective-permute-start.10 = (f32[5,16,4,128]{3,2,1,0:T(4,128)S(1)}, f32[5,16,4,128]{3,2,1,0:T(4,128)S(1)}, u32[]{:S(2)}, u32[]{:S(2)}) collective-permute-start(f32[5,16,4,128]{3,2,1,0:T(4,128)S(1)} %pad_maximum_fusion.8), channel_id=1, source_target_pairs={{4,0},{6,4},{2,6},{0,2},{5,1},{7,5},{3,7},{1,3},{12,8},{14,12},{10... | collective-permute-start | bytes 491528 | tf_op jit(solution)/shard_map/ppermute | solution.py:277
  49.8 16.9 %collective-permute-start.12 = (f32[5,4,32,128]{3,2,1,0:T(8,128)S(1)}, f32[5,4,32,128]{3,2,1,0:T(8,128)S(1)}, u32[]{:S(2)}, u32[]{:S(2)}) collective-permute-start(f32[5,4,32,128]{3,2,1,0:T(8,128)S(1)} %get-tuple-element.30), channel_id=1, source_target_pairs={{1,0},{5,4},{7,6},{3,2},{8,1},{12,5},{14,7},{10,3},{9,8},{13,12},{... | collective-permute-start | bytes 983048 | tf_op jit(solution)/shard_map/ppermute | solution.py:268
  51.7 16.3 %collective-permute-start.13 = (f32[5,8,32,128]{3,2,1,0:T(8,128)S(1)}, f32[5,8,32,128]{3,2,1,0:T(8,128)S(1)}, u32[]{:S(2)}, u32[]{:S(2)}) collective-permute-start(f32[5,8,32,128]{3,2,1,0:T(8,128)S(1)} %get-tuple-element.32.refs_1_), channel_id=1, source_target_pairs={{1,0},{5,4},{7,6},{3,2},{8,1},{12,5},{14,7},{10,3},{9,8},{13,12},{... | collective-permute-start | bytes 1966088 | tf_op jit(solution)/shard_map/ppermute | solution.py:268
  54.2 5.8 %collective-permute-start.9 = (f32[5,16,4,128]{3,2,1,0:T(4,128)S(1)}, f32[5,16,4,128]{3,2,1,0:T(4,128)S(1)}, u32[]{:S(2)}, u32[]{:S(2)}) collective-permute-start(f32[5,16,4,128]{3,2,1,0:T(4,128)S(1)} %pad_maximum_fusion.7), channel_id=1, source_target_pairs={{0,4},{4,6},{6,2},{2,0},{1,5},{5,7},{7,3},{3,1},{8,12},{12,14},{14... | collective-permute-start | bytes 491528 | tf_op jit(solution)/shard_map/ppermute | solution.py:276
  60.1 7.9 %collective-permute-start.11 = (f32[5,12,8,128]{3,2,1,0:T(8,128)S(1)}, f32[5,12,8,128]{3,2,1,0:T(8,128)S(1)}, u32[]{:S(2)}, u32[]{:S(2)}) collective-permute-start(f32[5,12,8,128]{3,2,1,0:T(8,128)S(1)} %pad_maximum_fusion.2), channel_id=1, source_target_pairs={{1,0},{5,4},{7,6},{3,2},{8,1},{12,5},{14,7},{10,3},{9,8},{13,12},{... | collective-permute-start | bytes 737288 | tf_op jit(solution)/shard_map/ppermute | solution.py:268
  73.5 6.0 %collective-permute-start.15 = (f32[5,16,4,128]{3,2,1,0:T(4,128)S(1)}, f32[5,16,4,128]{3,2,1,0:T(4,128)S(1)}, u32[]{:S(2)}, u32[]{:S(2)}) collective-permute-start(f32[5,16,4,128]{3,2,1,0:T(4,128)S(1)} %pad_maximum_fusion.10), channel_id=1, source_target_pairs={{4,0},{6,4},{2,6},{0,2},{5,1},{7,5},{3,7},{1,3},{12,8},{14,12},{10... | collective-permute-start | bytes 491528 | tf_op jit(solution)/shard_map/ppermute | solution.py:277
  74.8 17.0 %collective-permute-start.17 = (f32[5,4,32,128]{3,2,1,0:T(8,128)S(1)}, f32[5,4,32,128]{3,2,1,0:T(8,128)S(1)}, u32[]{:S(2)}, u32[]{:S(2)}) collective-permute-start(f32[5,4,32,128]{3,2,1,0:T(8,128)S(1)} %get-tuple-element.34), channel_id=1, source_target_pairs={{1,0},{5,4},{7,6},{3,2},{8,1},{12,5},{14,7},{10,3},{9,8},{13,12},{... | collective-permute-start | bytes 983048 | tf_op jit(solution)/shard_map/ppermute | solution.py:268
  76.7 16.3 %collective-permute-start.18 = (f32[5,8,32,128]{3,2,1,0:T(8,128)S(1)}, f32[5,8,32,128]{3,2,1,0:T(8,128)S(1)}, u32[]{:S(2)}, u32[]{:S(2)}) collective-permute-start(f32[5,8,32,128]{3,2,1,0:T(8,128)S(1)} %get-tuple-element.36.refs_1_), channel_id=1, source_target_pairs={{1,0},{5,4},{7,6},{3,2},{8,1},{12,5},{14,7},{10,3},{9,8},{13,12},{... | collective-permute-start | bytes 1966088 | tf_op jit(solution)/shard_map/ppermute | solution.py:268
  79.2 5.8 %collective-permute-start.14 = (f32[5,16,4,128]{3,2,1,0:T(4,128)S(1)}, f32[5,16,4,128]{3,2,1,0:T(4,128)S(1)}, u32[]{:S(2)}, u32[]{:S(2)}) collective-permute-start(f32[5,16,4,128]{3,2,1,0:T(4,128)S(1)} %pad_maximum_fusion.9), channel_id=1, source_target_pairs={{0,4},{4,6},{6,2},{2,0},{1,5},{5,7},{7,3},{3,1},{8,12},{12,14},{14... | collective-permute-start | bytes 491528 | tf_op jit(solution)/shard_map/ppermute | solution.py:276
  85.1 7.9 %collective-permute-start.16 = (f32[5,12,8,128]{3,2,1,0:T(8,128)S(1)}, f32[5,12,8,128]{3,2,1,0:T(8,128)S(1)}, u32[]{:S(2)}, u32[]{:S(2)}) collective-permute-start(f32[5,12,8,128]{3,2,1,0:T(8,128)S(1)} %pad_maximum_fusion.4), channel_id=1, source_target_pairs={{1,0},{5,4},{7,6},{3,2},{8,1},{12,5},{14,7},{10,3},{9,8},{13,12},{... | collective-permute-start | bytes 737288 | tf_op jit(solution)/shard_map/ppermute | solution.py:268
  98.5 5.9 %collective-permute-start.20 = (f32[5,16,4,128]{3,2,1,0:T(4,128)S(1)}, f32[5,16,4,128]{3,2,1,0:T(4,128)S(1)}, u32[]{:S(2)}, u32[]{:S(2)}) collective-permute-start(f32[5,16,4,128]{3,2,1,0:T(4,128)S(1)} %pad_maximum_fusion.12), channel_id=1, source_target_pairs={{4,0},{6,4},{2,6},{0,2},{5,1},{7,5},{3,7},{1,3},{12,8},{14,12},{10... | collective-permute-start | bytes 491528 | tf_op jit(solution)/shard_map/ppermute | solution.py:277
  98.7 16.8 %collective-permute-start.23 = (f32[5,4,32,128]{3,2,1,0:T(8,128)S(1)}, f32[5,4,32,128]{3,2,1,0:T(8,128)S(1)}, u32[]{:S(2)}, u32[]{:S(2)}) collective-permute-start(f32[5,4,32,128]{3,2,1,0:T(8,128)S(1)} %get-tuple-element.38), channel_id=1, source_target_pairs={{1,0},{5,4},{7,6},{3,2},{8,1},{12,5},{14,7},{10,3},{9,8},{13,12},{... | collective-permute-start | bytes 983048 | tf_op jit(solution)/shard_map/ppermute | solution.py:268
  100.6 16.3 %collective-permute-start.24 = (f32[5,8,32,128]{3,2,1,0:T(8,128)S(1)}, f32[5,8,32,128]{3,2,1,0:T(8,128)S(1)}, u32[]{:S(2)}, u32[]{:S(2)}) collective-permute-start(f32[5,8,32,128]{3,2,1,0:T(8,128)S(1)} %get-tuple-element.40.refs_1_), channel_id=1, source_target_pairs={{1,0},{5,4},{7,6},{3,2},{8,1},{12,5},{14,7},{10,3},{9,8},{13,12},{... | collective-permute-start | bytes 1966088 | tf_op jit(solution)/shard_map/ppermute | solution.py:268
  103.0 5.8 %collective-permute-start.19 = (f32[5,16,4,128]{3,2,1,0:T(4,128)S(1)}, f32[5,16,4,128]{3,2,1,0:T(4,128)S(1)}, u32[]{:S(2)}, u32[]{:S(2)}) collective-permute-start(f32[5,16,4,128]{3,2,1,0:T(4,128)S(1)} %pad_maximum_fusion.11), channel_id=1, source_target_pairs={{0,4},{4,6},{6,2},{2,0},{1,5},{5,7},{7,3},{3,1},{8,12},{12,14},{14... | collective-permute-start | bytes 491528 | tf_op jit(solution)/shard_map/ppermute | solution.py:276
  108.9 7.9 %collective-permute-start.22 = (f32[5,12,8,128]{3,2,1,0:T(8,128)S(1)}, f32[5,12,8,128]{3,2,1,0:T(8,128)S(1)}, u32[]{:S(2)}, u32[]{:S(2)}) collective-permute-start(f32[5,12,8,128]{3,2,1,0:T(8,128)S(1)} %pad_maximum_fusion.6), channel_id=1, source_target_pairs={{1,0},{5,4},{7,6},{3,2},{8,1},{12,5},{14,7},{10,3},{9,8},{13,12},{... | collective-permute-start | bytes 737288 | tf_op jit(solution)/shard_map/ppermute | solution.py:268
  120.2 18.9 %collective-permute-start.25 = (f32[5,6,32,128]{3,2,1,0:T(8,128)S(1)}, f32[5,6,32,128]{3,2,1,0:T(8,128)S(1)}, u32[]{:S(2)}, u32[]{:S(2)}) collective-permute-start(f32[5,6,32,128]{3,2,1,0:T(8,128)S(1)} %get-tuple-element.44), channel_id=1, source_target_pairs={{0,0},{4,1},{6,2},{2,3},{1,4},{5,5},{7,6},{3,7},{8,8},{12,9},{14,1... | collective-permute-start | bytes 1474568 | tf_op jit(solution)/shard_map/ppermute | solution.py:268
  125.3 13.8 %collective-permute-start.26 = (f32[5,6,32,128]{3,2,1,0:T(8,128)S(1)}, f32[5,6,32,128]{3,2,1,0:T(8,128)S(1)}, u32[]{:S(2)}, u32[]{:S(2)}) collective-permute-start(f32[5,6,32,128]{3,2,1,0:T(8,128)S(1)} %part.17), channel_id=1, source_target_pairs={{0,0},{4,1},{6,2},{2,3},{1,4},{5,5},{7,6},{3,7},{8,8},{12,9},{14,1... | collective-permute-start | bytes 1474568 | tf_op jit(solution)/shard_map/ppermute | solution.py:268
  128.9 10.1 %collective-permute-start.21 = (f32[5,4,32,128]{3,2,1,0:T(8,128)S(1)}, f32[5,4,32,128]{3,2,1,0:T(8,128)S(1)}, u32[]{:S(2)}, u32[]{:S(2)}) collective-permute-start(f32[5,4,32,128]{3,2,1,0:T(8,128)S(1)} %get-tuple-element.42), channel_id=1, source_target_pairs={{0,0},{4,1},{6,2},{2,3},{1,4},{5,5},{7,6},{3,7},{8,8},{12,9},{14,1... | collective-permute-start | bytes 983048 | tf_op jit(solution)/shard_map/ppermute | solution.py:268
  (1 other events, 10.9 us)
